TPU v7x, 32 devices: a whole 2x2x4 slice. The times are simulated.
32 devices in a mesh: grp: 2 (over y), dev: 16 (over z, x, core).
Axes of the slice: x: 2, y: 2, z: 4, core: 2. Of those that a mesh axis runs over, the one named last changes fastest.
Arguments:
- spectra: bfloat16 [512, 2, 2048], P(('grp', 'dev')), may hold values from -6 to 6
- stack_in: bfloat16 [2, 256, 512, 128], P(None, None, ('grp', 'dev')), may hold values from -6 to 6
- plan: int32 [2], replicated, may hold values from 0 to 1
- seg_lengths: int32 [16], replicated, may hold values from 1 to 64, 512 in all
- taps: float32 [9], replicated, may hold values from -3 to 3
Outputs:
- stack: float32 [2, 256, 512, 128], P(None, None, ('grp', 'dev'))
- filtered: float32 [2, 256, 512, 128], P(None, None, ('grp', 'dev'))
All inputs are finite; a program needn't handle non-finite values.
Results may differ from a plain program's by a relative error of at most 0.0026.
Values may be sent and summed in bfloat16 or wider, within the bound.
No kernel may reach another device: no remote copies, remote signals or barrier semaphores. Data moves between devices by JAX's collectives and lax.ppermute only.
A program may use at most 64 MiB of HBM per device.

v0:
```python
import math

import jax
import jax.numpy as jnp
from jax import lax
from jax.sharding import PartitionSpec as P


def from_root(value, axis, source):
    kept = jnp.where(lax.axis_index(axis) == source, value, 0).astype(value.dtype)
    return lax.psum(kept, axis)


def extended_2(block, sides, width):
    for axis, dim in sides:
        count = lax.axis_size(axis)
        forward = [(i, i + 1) for i in range(count - 1)]
        backward = [(target, source) for source, target in forward]
        low = lax.ppermute(
            lax.slice_in_dim(block, block.shape[dim] - width, None, axis=dim), axis, forward
        )
        high = lax.ppermute(lax.slice_in_dim(block, 0, width, axis=dim), axis, backward)
        block = jnp.concatenate([low, block, high], axis=dim)
    return block


def whiten(spectra):
    real_part = spectra[:, 0, :].astype(jnp.float32)
    imag_part = spectra[:, 1, :].astype(jnp.float32)
    magnitude = jnp.sqrt(real_part * real_part + imag_part * imag_part)
    factor = 1.0 / jnp.maximum(magnitude, 0.25)
    return jnp.stack([real_part * factor, imag_part * factor], axis=1).astype(jnp.bfloat16)


def make_table(freqs, lags):
    bins = jnp.arange(freqs, dtype=jnp.int32)[:, None]
    shifts = jnp.arange(lags, dtype=jnp.int32)[None, :] - lags // 2
    modulus = bins * shifts % (2 * freqs)
    angle = modulus.astype(jnp.float32) * (math.pi / freqs)
    scale_value = 1.0 / math.sqrt(freqs)
    table = jnp.concatenate([jnp.cos(angle), -jnp.sin(angle)], axis=0) * scale_value
    return table.astype(jnp.bfloat16)


def cross_block(sources, receivers, table):
    src_re = sources[:, 0, :].astype(jnp.float32)[:, None, :]
    src_im = sources[:, 1, :].astype(jnp.float32)[:, None, :]
    rec_re = receivers[:, 0, :].astype(jnp.float32)[None, :, :]
    rec_im = receivers[:, 1, :].astype(jnp.float32)[None, :, :]
    cross_re = src_re * rec_re + src_im * rec_im
    cross_im = src_im * rec_re - src_re * rec_im
    cross = jnp.concatenate([cross_re, cross_im], axis=-1).astype(jnp.bfloat16)
    rows = sources.shape[0] * receivers.shape[0]
    flat = cross.reshape(rows, cross.shape[-1])
    result = jnp.dot(flat, table, preferred_element_type=jnp.float32)
    return result.reshape(sources.shape[0], receivers.shape[0], table.shape[1])


def segment_of(channel_ids, seg_lengths):
    bounds = jnp.cumsum(seg_lengths)[:-1]
    return jnp.sum((channel_ids[:, None] >= bounds[None, :]).astype(jnp.int32), axis=1)


def mixing_weights(seg_ids, taps, count):
    width = (taps.shape[0] - 1) // 2
    centre = seg_ids[width : width + count]
    columns = []
    for offset in range(taps.shape[0]):
        same = (seg_ids[offset : offset + count] == centre).astype(jnp.float32)
        columns.append(taps[offset] * same)
    return jnp.stack(columns, axis=1)


def apply_filter(extended, mixing, dim, count):
    total = jnp.zeros(extended.shape[:dim] + (count,) + extended.shape[dim + 1 :], jnp.float32)
    for offset in range(mixing.shape[1]):
        part = lax.slice_in_dim(extended, offset, offset + count, axis=dim)
        shape = [1] * extended.ndim
        shape[dim] = count
        total = total + mixing[:, offset].reshape(shape) * part
    return total


def shards(spectra, stack_in, plan, seg_lengths, taps):
    shard = spectra.shape[0]
    freqs = spectra.shape[2]
    steps = stack_in.shape[0]
    source_count = stack_in.shape[1]
    lags = stack_in.shape[3]
    width = (taps.shape[0] - 1) // 2
    group_channels = lax.axis_size("dev") * shard
    own = whiten(spectra)
    table = make_table(freqs, lags)
    block_rows = min(source_count, max(1, 512 // shard))
    start_channel = lax.axis_index(("grp", "dev")) * shard
    channel_ids = start_channel + jnp.arange(shard + 2 * width, dtype=jnp.int32) - width
    seg_ids = segment_of(channel_ids, seg_lengths)
    mixing = mixing_weights(seg_ids, taps, shard)
    stacks = []
    filtered_list = []
    for step in range(steps):
        first = plan[step] * source_count
        owner = first // group_channels
        offset = first % group_channels
        whole = lax.all_gather(own, "dev", axis=0, tiled=True)
        piece = lax.dynamic_slice_in_dim(whole, offset, source_count, 0)
        sources = from_root(piece, "grp", owner)
        grouped = sources.reshape(source_count // block_rows, block_rows, 2, freqs)
        corr = lax.map(lambda block: cross_block(block, own, table), grouped)
        corr = corr.reshape(source_count, shard, lags)
        updated = stack_in[step].astype(jnp.float32) + corr
        stacks.append(updated)
        extended = extended_2(updated, ((("grp", "dev"), 1),), width)
        filtered_list.append(apply_filter(extended, mixing, 1, shard))
    stack = jnp.stack(stacks, axis=0)
    filtered = jnp.stack(filtered_list, axis=0)
    return (stack, filtered)


def solution(mesh):
    placed = (P(("grp", "dev"), None, None), P(None, None, ("grp", "dev"), None), P(), P(), P())
    return jax.shard_map(
        shards,
        mesh=mesh,
        in_specs=placed,
        out_specs=(P(None, None, ("grp", "dev"), None), P(None, None, ("grp", "dev"), None)),
        check_vma=False,
    )
```

profile of v0, /device:TPU:1, one launch (start us, length us, event | category | flops | bytes accessed | tf_op | source)
XLA Modules:
  0.0 273.0 jit_solution(8880762887707342477)
XLA Ops:
  12.0 42.2 %all-gather.2.cloned.1.call-done = bf16[256,2,2048]{2,0,1:T(8,128)(2,1)} async-done(((bf16[16,2,2048]{2,0,1:T(8,128)(2,1)}), bf16[256,2,2048]{2,0,1:T(8,128)(2,1)}) %all-gather.2.cloned.1.call-update) | async-done | bytes 2097168 | tf_op jit(solution)/shard_map/all_gather | solution.py:105
  54.1 1.9 broadcast_select_fusion.1
  56.0 1.5 copy.19
  57.4 1.5 copy.20
  61.9 3.9 %compare_select_fusion.7 = (f32[16]{0:T(128)S(1)}, f32[16]{0:T(128)S(1)}, f32[16]{0:T(128)S(1)}, f32[16]{0:T(128)S(1)}, f32[16]{0:T(128)S(1)}, /*index=5*/f32[16]{0:T(128)S(1)}) fusion(s32[24]{0:T(128)S(1)} %convert_reduce_fusion, f32[]{:T(128)} %bitcast.21, f32[]{:T(128)} %bitcast.30, f32[]{:T(128)} %bitcast.29, f32[]{:T(128)} %bitcast.28, f32[]{:T(128)} %bitcast.26, ...), kind=kLoop, calls=%fused_computation.151 | loop fusion | flops 192 | bytes 856 | tf_op jit(solution)/shard_map/mul | solution.py:70
  65.8 4.1 %fusion.83 = (f32[2048,128]{1,0:T(8,128)S(1)}, f32[2048,128]{1,0:T(8,128)S(1)}) fusion(s32[128]{0:T(128)S(1)} %iota_add_fusion), kind=kLoop, calls=%fused_computation.130 | loop fusion | flops 3932160 | bytes 2097664 | tf_op jit(solution)/shard_map/cos | solution.py:41
  70.2 95.0 %all-reduce.3.cloned.1.call-done = (bf16[8,32,2,2048]{3,1,2,0:T(8,128)(2,1)}, bf16[8,32,2,2048]{3,1,2,0:T(8,128)(2,1)}) async-done(((bf16[8,32,2,2048]{3,1,2,0:T(8,128)(2,1)}, bf16[8,32,2,2048]{3,1,2,0:T(8,128)(2,1)}), (bf16[8,32,2,2048]{3,1,2,0:T(8,128)(2,1)}, bf16[8,32,2,2048]{3,1,2,0:T(8,128)(2,1)})) %all-reduce.3.cloned.1.call-update) | async-done | bytes 4194320 | tf_op jit(solution)/shard_map/psum | solution.py:11
  165.4 29.9 %while.21 = (s32[]{:T(128)}, f32[8,32,16,128]{3,2,1,0:T(8,128)S(1)}, bf16[8,32,2,2048]{3,1,2,0:T(8,128)(2,1)}, bf16[16,2,2048]{2,0,1:T(8,128)(2,1)S(1)}, bf16[4096,128]{1,0:T(8,128)(2,1)S(1)}, /*index=5*/s32[]{:T(128)}) while((s32[]{:T(128)}, f32[8,32,16,128]{3,2,1,0:T(8,128)S(1)}, bf16[8,32,2,2048]{3,1,2,0:T(8,128)(2,1)}, ...), condition=%wide.region_5.6_spmd, body=%wide.region_4.5_spmd.sunk | while | flops 553844736 | bytes 12189773 | solution.py:109
  166.4 1.4 add_convert_fusion.5
  170.2 1.4 add_convert_fusion.5
  173.9 1.4 add_convert_fusion.5
  177.7 1.4 add_convert_fusion.5
  181.4 1.4 add_convert_fusion.5
  185.1 1.4 add_convert_fusion.5
  188.9 1.4 add_convert_fusion.5
  192.6 1.4 add_convert_fusion.5
  196.8 29.9 %while.20 = (s32[]{:T(128)}, f32[8,32,16,128]{3,2,1,0:T(8,128)S(1)}, bf16[8,32,2,2048]{3,1,2,0:T(8,128)(2,1)}, bf16[16,2,2048]{2,0,1:T(8,128)(2,1)S(1)}, bf16[4096,128]{1,0:T(8,128)(2,1)S(1)}, /*index=5*/s32[]{:T(128)}) while((s32[]{:T(128)}, f32[8,32,16,128]{3,2,1,0:T(8,128)S(1)}, bf16[8,32,2,2048]{3,1,2,0:T(8,128)(2,1)}, ...), condition=%wide.region_2.3_spmd, body=%wide.region_1.2_spmd.sunk | while | flops 553844736 | bytes 12189773 | solution.py:109
  197.9 1.4 add_convert_fusion.4
  205.4 1.4 add_convert_fusion.4
  209.1 1.4 add_convert_fusion.4
  212.8 1.4 add_convert_fusion.4
  226.8 2.7 fusion.28
  229.7 4.1 %collective-permute-start = (f32[256,4,128]{2,1,0:T(4,128)S(1)}, f32[256,4,128]{2,1,0:T(4,128)S(1)}, u32[]{:S(2)}, u32[]{:S(2)}) collective-permute-start(f32[256,4,128]{2,1,0:T(4,128)S(1)} %get-tuple-element.92), channel_id=1, source_target_pairs={{0,1},{1,2},{2,3},{3,4},{4,5},{5,6},{6,7},{7,8},{8,9},{9,10},{10,1... | collective-permute-start | bytes 1572872 | tf_op jit(solution)/shard_map/ppermute | solution.py:19
  233.8 2.1 collective-permute-start.1
  236.1 3.6 %collective-permute-start.2 = (f32[256,4,128]{2,1,0:T(4,128)S(1)}, f32[256,4,128]{2,1,0:T(4,128)S(1)}, u32[]{:S(2)}, u32[]{:S(2)}) collective-permute-start(f32[256,4,128]{2,1,0:T(4,128)S(1)} %get-tuple-element.96), channel_id=1, source_target_pairs={{0,1},{1,2},{2,3},{3,4},{4,5},{5,6},{6,7},{7,8},{8,9},{9,10},{10,1... | collective-permute-start | bytes 1572872 | tf_op jit(solution)/shard_map/ppermute | solution.py:19
  239.7 1.9 collective-permute-start.3
  242.1 2.3 pad_maximum_fusion
  245.5 8.8 %collective-permute-done.1 = f32[256,4,128]{2,1,0:T(4,128)S(1)} collective-permute-done((f32[256,4,128]{2,1,0:T(4,128)S(1)}, f32[256,4,128]{2,1,0:T(4,128)S(1)}, u32[]{:S(2)}, u32[]{:S(2)}) %collective-permute-start.1) | collective-permute-done | bytes 524320 | tf_op jit(solution)/shard_map/ppermute | solution.py:22
  254.3 3.9 %fusion.55 = f32[1,256,16,128]{3,2,1,0:T(8,128)S(1)} fusion(f32[256,16,128]{2,1,0:T(8,128)S(1)} %get-tuple-element.94, f32[256,4,128]{2,1,0:T(4,128)S(1)} %collective-permute-done.1, f32[256,4,128]{2,1,0:T(4,128)S(1)} %collective-permute-done, f32[16]{0:T(128)S(1)} %get-tuple-element.122, f32[16]{0:T(128)S(1)} %get-tuple-element.107, ...), kind=kLoop, calls=%fused_computation.91 | loop fusion | flops 13107200 | bytes 5243396 | tf_op jit(solution)/shard_map/stack | solution.py:116
  258.2 1.7 collective-permute-done.3
  259.9 3.9 %fusion.34 = f32[1,256,16,128]{3,2,1,0:T(8,128)S(1)} fusion(f32[256,16,128]{2,1,0:T(8,128)S(1)} %get-tuple-element.95, f32[256,4,128]{2,1,0:T(4,128)S(1)} %collective-permute-done.3, f32[256,4,128]{2,1,0:T(4,128)S(1)} %collective-permute-done.2, f32[16]{0:T(128)S(1)} %get-tuple-element.122, f32[16]{0:T(128)S(1)} %get-tuple-element.107, ...), kind=kLoop, calls=%fused_computation.70 | loop fusion | flops 13107200 | bytes 5243396 | tf_op jit(solution)/shard_map/stack | solution.py:116
  263.8 2.3 pad_maximum_fusion.1
  (104 shorter events, 52.2 us)
Async XLA Ops:
  7.2 47.0 %all-gather.2.cloned.1.call-start = ((), (), s32[]{:S(2)}) async-start(), calls=%async_computation | async-start | bytes 2228224 | tf_op jit(solution)/shard_map/all_gather | solution.py:105
  9.2 155.9 %all-reduce.3.cloned.1.call-start = ((), (), s32[]{:S(2)}) async-start(), calls=%async_computation.1 | async-start | bytes 8388608 | tf_op jit(solution)/shard_map/psum | solution.py:11
  58.9 0.7 copy-start.5
  58.9 0.9 copy-start.4
  70.0 95.4 %copy-start = (bf16[16,2,2048]{2,0,1:T(8,128)(2,1)S(1)}, bf16[16,2,2048]{2,0,1:T(8,128)(2,1)}, u32[]{:S(2)}) copy-start(bf16[16,2,2048]{2,0,1:T(8,128)(2,1)} %pad_maximum_fusion.6) | copy-start | bytes 393220
  195.3 1.3 copy-start.1
  229.5 12.2 %copy-start.2 = (f32[8,32,16,128]{3,2,1,0:T(8,128)S(1)}, f32[8,32,16,128]{3,2,1,0:T(8,128)}, u32[]{:S(2)}) copy-start(f32[8,32,16,128]{3,2,1,0:T(8,128)} %copy-done.1) | copy-start | bytes 6291460
  229.5 12.2 %copy-start.3 = (bf16[2,256,16,128]{3,2,1,0:T(8,128)(2,1)S(1)}, bf16[2,256,16,128]{3,2,1,0:T(8,128)(2,1)}, u32[]{:S(2)}) copy-start(bf16[2,256,16,128]{3,2,1,0:T(8,128)(2,1)} %param.10) | copy-start | bytes 6291460
  229.7 15.8 %collective-permute-start = (f32[256,4,128]{2,1,0:T(4,128)S(1)}, f32[256,4,128]{2,1,0:T(4,128)S(1)}, u32[]{:S(2)}, u32[]{:S(2)}) collective-permute-start(f32[256,4,128]{2,1,0:T(4,128)S(1)} %get-tuple-element.92), channel_id=1, source_target_pairs={{0,1},{1,2},{2,3},{3,4},{4,5},{5,6},{6,7},{7,8},{8,9},{9,10},{10,1... | collective-permute-start | bytes 1572872 | tf_op jit(solution)/shard_map/ppermute | solution.py:19
  233.8 20.5 %collective-permute-start.1 = (f32[256,4,128]{2,1,0:T(4,128)S(1)}, f32[256,4,128]{2,1,0:T(4,128)S(1)}, u32[]{:S(2)}, u32[]{:S(2)}) collective-permute-start(f32[256,4,128]{2,1,0:T(4,128)S(1)} %get-tuple-element.93), channel_id=1, source_target_pairs={{1,0},{2,1},{3,2},{4,3},{5,4},{6,5},{7,6},{8,7},{9,8},{10,9},{11,1... | collective-permute-start | bytes 1572872 | tf_op jit(solution)/shard_map/ppermute | solution.py:22
  236.1 22.2 %collective-permute-start.2 = (f32[256,4,128]{2,1,0:T(4,128)S(1)}, f32[256,4,128]{2,1,0:T(4,128)S(1)}, u32[]{:S(2)}, u32[]{:S(2)}) collective-permute-start(f32[256,4,128]{2,1,0:T(4,128)S(1)} %get-tuple-element.96), channel_id=1, source_target_pairs={{0,1},{1,2},{2,3},{3,4},{4,5},{5,6},{6,7},{7,8},{8,9},{9,10},{10,1... | collective-permute-start | bytes 1572872 | tf_op jit(solution)/shard_map/ppermute | solution.py:19
  239.7 20.2 %collective-permute-start.3 = (f32[256,4,128]{2,1,0:T(4,128)S(1)}, f32[256,4,128]{2,1,0:T(4,128)S(1)}, u32[]{:S(2)}, u32[]{:S(2)}) collective-permute-start(f32[256,4,128]{2,1,0:T(4,128)S(1)} %get-tuple-element.97), channel_id=1, source_target_pairs={{1,0},{2,1},{3,2},{4,3},{5,4},{6,5},{7,6},{8,7},{9,8},{10,9},{11,1... | collective-permute-start | bytes 1572872 | tf_op jit(solution)/shard_map/ppermute | solution.py:22
Sparse Core Ops, SparseCore 0:
  10.2 43.9 all-gather.1
  59.1 106.0 all-reduce.2
where the time goes:
time: 274 us; the launch traced here: 273 us
  waiting for transfers between devices  149 us (54%)
  other arithmetic  51.5 us (19%)
  local copies, waits for them, and re-layouts  24.5 us (9%)
  matrix products  20 us (7%)
  between operations  15.6 us (6%)
  starting transfers between devices  11.8 us (4%)
    psum x1, waiting for transfers between devices, from_root(): return lax.psum(kept, axis)  95 us
    all_gather x1, waiting for transfers between devices, shards(): whole = lax.all_gather(own, 'dev', axis=0, tiled=True)  42.2 us
    another operation x18, other arithmetic  22.8 us
    dot_general x16, matrix products, cross_block(): result = jnp.dot(flat, table, preferred_element_type=jnp.float32)  20 us
    squeeze x16, local copies, waits for them, and re-layouts, shards(): corr = lax.map(lambda block: cross_block(block, own, table), grouped)  15.5 us
    ppermute x2, waiting for transfers between devices, extended_2(): lax.ppermute(lax.slice_in_dim(block, 0, width, axis=dim), axis, backward)  10.5 us
    another operation x3, other arithmetic, shards(): filtered = jnp.stack(filtered_list, axis=0)  10.1 us
    ppermute x2, starting transfers between devices, extended_2(): lax.ppermute(lax.slice_in_dim(block, block.shape[dim] - width, None, axis...  7.73 us
  transfers between devices with their start and end apart: 6, of which 5 were waited for; matrix products, arithmetic and copies ran while one was open for 7% of the time, Pallas kernels for 0%

commit v1 on v0

v1 whole, which is shorter than its diff:
```python
import functools
import math

import jax
import jax.numpy as jnp
import ml_dtypes
import numpy as np
from jax import lax
from jax.experimental import pallas as pl
from jax.experimental.pallas import tpu as pltpu
from jax.sharding import PartitionSpec as P

AXES = ("grp", "dev")
FILL = 512


def whiten(spectra):
    real_part = spectra[:, 0, :].astype(jnp.float32)
    imag_part = spectra[:, 1, :].astype(jnp.float32)
    magnitude = jnp.sqrt(real_part * real_part + imag_part * imag_part)
    factor = 1.0 / jnp.maximum(magnitude, 0.25)
    pair = jnp.concatenate([real_part * factor, imag_part * factor], axis=1)
    return pair.astype(jnp.bfloat16)


def make_table(freqs, lags):
    bins = np.arange(freqs, dtype=np.int64)[None, :]
    shifts = np.arange(lags, dtype=np.int64)[:, None] - lags // 2
    modulus = (bins * shifts) % (2 * freqs)
    angle = modulus.astype(np.float64) * (math.pi / freqs)
    table = np.concatenate([np.cos(angle), -np.sin(angle)], axis=1) / math.sqrt(freqs)
    return jnp.asarray(table.astype(np.float32).astype(ml_dtypes.bfloat16))


def segment_of(channel_ids, seg_lengths):
    bounds = jnp.cumsum(seg_lengths)[:-1]
    return jnp.sum((channel_ids[:, None] >= bounds[None, :]).astype(jnp.int32), axis=1)


def mixing_weights(seg_ids, taps, count):
    width = (taps.shape[0] - 1) // 2
    centre = seg_ids[width : width + count]
    columns = []
    for offset in range(taps.shape[0]):
        same = (seg_ids[offset : offset + count] == centre).astype(jnp.float32)
        columns.append(taps[offset] * same)
    return jnp.stack(columns, axis=0)


def weights_kernel(receivers, table, weights):
    count, lags, freqs = receivers.shape[0], table.shape[0], table.shape[1] // 2
    fill = min(FILL, freqs)

    def body(step, _):
        first = pl.multiple_of(step * fill, fill)
        low, high = pl.ds(first, fill), pl.ds(freqs + first, fill)
        cosine = table[:, low].astype(jnp.float32)
        sine = table[:, high].astype(jnp.float32)
        for c in range(count):
            real_part = receivers[pl.ds(c, 1), low].astype(jnp.float32)
            imag_part = receivers[pl.ds(c, 1), high].astype(jnp.float32)
            rows = pl.ds(c * lags, lags)
            weights[rows, low] = (real_part * cosine - imag_part * sine).astype(jnp.bfloat16)
            weights[rows, high] = (imag_part * cosine + real_part * sine).astype(jnp.bfloat16)
        return 0

    lax.fori_loop(0, freqs // fill, body, 0)


def make_weights(receivers, table):
    count, bins = receivers.shape
    lags = table.shape[0]
    return pl.pallas_call(
        weights_kernel,
        out_shape=pltpu.VMEM((count * lags, bins), jnp.bfloat16),
        in_specs=[pl.BlockSpec(memory_space=pltpu.VMEM)] * 2,
        out_specs=pl.BlockSpec(memory_space=pltpu.VMEM),
        compiler_params=pltpu.CompilerParams(vmem_limit_bytes=8 << 20),
        cost_estimate=pl.CostEstimate(
            flops=3 * count * lags * bins, bytes_accessed=2 * count * lags * bins, transcendentals=0
        ),
        name="make_weights",
    )(receivers, table)


def block_kernel(unit, parts, info, mix, *refs):
    sources = refs[:parts]
    weights, kept = refs[parts], refs[parts + 1]
    stack_out, filtered_out = refs[-7], refs[-6]
    lhs, corr, stack_buf, filtered_buf, sems = refs[-5:]
    rows = lhs.shape[0]
    units = rows // unit
    steps, _, reach, lags = kept.shape
    taps, shard, _ = mix.shape
    width = (taps - 1) // 2
    first = 0
    for part in sources:
        lhs[pl.ds(first, part.shape[0]), :] = part[...]
        first += part.shape[0]
    group = 4
    columns = group * lags

    def product(step, _):
        at = pl.multiple_of(step * columns, columns)
        out = lax.dot_general(
            lhs[...],
            weights[pl.ds(at, columns), :],
            (((1,), (1,)), ((), ())),
            preferred_element_type=jnp.float32,
        )
        for j in range(group):
            channel = step * group + j
            corr[pl.ds(channel, rows, stride=reach), :] = out[:, j * lags : (j + 1) * lags]
        return 0

    lax.fori_loop(0, reach // group, product, 0)

    def copies(slot, step, row):
        return (
            pltpu.make_async_copy(
                stack_buf.at[slot], stack_out.at[step, pl.ds(row, unit)], sems.at[0, slot]
            ),
            pltpu.make_async_copy(
                filtered_buf.at[slot], filtered_out.at[step, pl.ds(row, unit)], sems.at[1, slot]
            ),
        )

    def finish(slot):
        for copy in copies(slot, 0, 0):
            copy.wait()

    def visit(number, used):
        u, step = number // steps, number % steps
        row = info[steps + units + u]

        def work(used):
            slot = used % 2

            @pl.when(used >= 2)
            def _():
                finish(slot)

            for i in range(unit):
                at = pl.multiple_of((u * unit + i) * reach, reach)
                whole = corr[pl.ds(at, reach), :] + kept[step, row + i].astype(jnp.float32)
                stack_buf[slot, i] = whole[:shard]
                total = mix[width] * whole[:shard]
                for offset in range(-width, width + 1):
                    if offset:
                        moved = pltpu.roll(whole, (-offset) % reach, 0)[:shard]
                        total = total + mix[width + offset] * moved
                filtered_buf[slot, i] = total
            for copy in copies(slot, step, row):
                copy.start()
            return used + 1

        return lax.cond(info[step] == info[steps + u], work, lambda used: used, used)

    used = lax.fori_loop(0, units * steps, visit, 0)

    @pl.when(used >= 1)
    def _():
        finish((used - 1) % 2)

    @pl.when(used >= 2)
    def _():
        finish(used % 2)


def block(sources, weights, kept, mix, info, unit, outs, out_shape):
    rows = sum(part.shape[0] for part in sources)
    steps, count, reach, lags = kept.shape
    taps, shard, _ = mix.shape
    bins = weights.shape[1]
    vmem, anywhere = pl.BlockSpec(memory_space=pltpu.VMEM), pl.BlockSpec(memory_space=pl.ANY)
    carried = list(outs)
    before = 2 + len(sources) + 2
    return pl.pallas_call(
        functools.partial(block_kernel, unit, len(sources)),
        out_shape=(out_shape, out_shape),
        in_specs=[pl.BlockSpec(memory_space=pltpu.SMEM)]
        + [vmem] * (1 + len(sources) + 2)
        + [anywhere] * len(carried),
        out_specs=(anywhere, anywhere),
        scratch_shapes=[
            pltpu.VMEM((rows, bins), jnp.bfloat16),
            pltpu.VMEM((rows * reach, lags), jnp.float32),
            pltpu.VMEM((2, unit, shard, lags), jnp.float32),
            pltpu.VMEM((2, unit, shard, lags), jnp.float32),
            pltpu.SemaphoreType.DMA((2, 2)),
        ],
        input_output_aliases={before: 0, before + 1: 1} if carried else {},
        compiler_params=pltpu.CompilerParams(vmem_limit_bytes=14 << 20),
        cost_estimate=pl.CostEstimate(
            flops=2 * rows * bins * reach * lags,
            bytes_accessed=8 * rows * shard * lags,
            transcendentals=0,
        ),
        name="block",
    )(info, mix, *sources, weights, kept, *carried)


def pairs(groups, devs, move):
    lines = devs // 4
    listed = []
    for g in range(groups):
        for line in range(lines):
            for side in range(2):
                for core in range(2):
                    h, other, flank, die = move(g, line, side, core)
                    listed.append(
                        (
                            g * devs + (line * 2 + side) * 2 + core,
                            h * devs + (other * 2 + flank) * 2 + die,
                        )
                    )
    return listed


def gather_small(own):
    groups, devs = lax.axis_size("grp"), lax.axis_size("dev")
    lines = devs // 4
    g, d = lax.axis_index("grp"), lax.axis_index("dev")
    line, side, core = d // 4, (d // 2) % 2, d % 2

    def send(value, move):
        return lax.ppermute(value, AXES, pairs(groups, devs, move))

    held = [own]
    for k in range(1, lines):
        held.append(send(own, lambda h, n, s, c: (h, (n + k) % lines, s, c)))
    first = jnp.concatenate(held, axis=0)
    second = send(first, lambda h, n, s, c: (h, n, 1 - s, c) if c == 0 else (1 - h, n, s, c))
    near = jnp.concatenate([first, second], axis=0)
    far = send(near, lambda h, n, s, c: (h, n, 1 - s, c) if c == 1 else (1 - h, n, s, c))
    near_other = send(near, lambda h, n, s, c: (h, n, s, 1 - c))
    far_other = send(far, lambda h, n, s, c: (h, n, s, 1 - c))

    def owners(core, far):
        listed = []
        for j in range(2):
            flip_side = jnp.where(core == 0, j, far)
            flip_group = jnp.where(core == 0, far, j)
            for k in range(lines):
                at_group = jnp.bitwise_xor(g, flip_group)
                at_side = jnp.bitwise_xor(side, flip_side)
                at_line = (line - k + lines) % lines
                listed.append(at_group * devs + (at_line * 2 + at_side) * 2 + core)
        return listed

    return (
        ((near, near_other), jnp.stack(owners(core, 0) + owners(1 - core, 0))),
        ((far, far_other), jnp.stack(owners(core, 1) + owners(1 - core, 1))),
    )


def shards(spectra, stack_in, plan, seg_lengths, taps):
    shard, _, freqs = spectra.shape
    steps, source_count, _, lags = stack_in.shape
    width = (taps.shape[0] - 1) // 2
    groups, devs = lax.axis_size("grp"), lax.axis_size("dev")
    total = groups * devs
    group_channels = devs * shard
    reach = shard + 2 * width

    own = whiten(spectra)
    start_channel = lax.axis_index(AXES) * shard
    channel_ids = start_channel + jnp.arange(reach, dtype=jnp.int32) - width
    mixing = mixing_weights(segment_of(channel_ids, seg_lengths), taps, shard)
    mix = jnp.broadcast_to(mixing[:, :, None], mixing.shape + (lags,))

    edge = steps * source_count * width

    def packed(first):
        stacks = lax.slice_in_dim(stack_in, first, first + width, axis=2)
        raw = lax.slice_in_dim(spectra, first, first + width, axis=0)
        return jnp.concatenate([stacks.reshape(edge, lags), raw.reshape(-1, lags)], axis=0)

    low = lax.ppermute(packed(shard - width), AXES, [(i, i + 1) for i in range(total - 1)])
    high = lax.ppermute(packed(0), AXES, [(i + 1, i) for i in range(total - 1)])

    def stacks_of(edges):
        return edges[:edge].reshape(steps, source_count, width, lags)

    def white_of(edges):
        return whiten(edges[edge:].reshape(width, 2, freqs))

    kept = jnp.concatenate([stack_in, stacks_of(high), stacks_of(low)], axis=2)
    receivers = jnp.concatenate([own, white_of(high), white_of(low)], axis=0)
    weights = make_weights(receivers, make_table(freqs, lags))

    out_shape = jax.ShapeDtypeStruct((steps, source_count, shard, lags), jnp.float32)
    outs = ()
    if groups == 2 and devs % 4 == 0 and total * shard == 2 * source_count:
        for sources, owners in gather_small(own):
            channels = owners * shard
            info = jnp.concatenate([plan, channels // source_count, channels % source_count])
            outs = block(
                sources, weights, kept, mix, info.astype(jnp.int32), shard, outs, out_shape
            )
        return outs
    for step in range(steps):
        first = plan[step] * source_count
        mine = jnp.where(lax.axis_index("grp") == first // group_channels, own, 0)
        piece = lax.psum(mine.astype(own.dtype), "grp")
        whole = lax.all_gather(piece, "dev", axis=0, tiled=True)
        sources = lax.dynamic_slice_in_dim(whole, first % group_channels, source_count, 0)
        units = source_count // shard
        info = jnp.concatenate(
            [
                jnp.arange(steps, dtype=jnp.int32),
                jnp.full((units,), step, jnp.int32),
                jnp.arange(units, dtype=jnp.int32) * shard,
            ]
        )
        outs = block((sources,), weights, kept, mix, info, shard, outs, out_shape)
    return outs


def solution(mesh):
    placed = (P(AXES, None, None), P(None, None, AXES, None), P(), P(), P())
    return jax.shard_map(
        shards,
        mesh=mesh,
        in_specs=placed,
        out_specs=(P(None, None, AXES, None), P(None, None, AXES, None)),
        check_vma=False,
    )
```

time: 274 us -> 113 us (0.41)
  waiting for transfers between devices: 149 us -> 11.8 us
  other arithmetic: 51.5 us -> 9.27 us
  Pallas kernels: 0 us -> 36.8 us
  matrix products: 20 us -> 0 us
  starting transfers between devices: 11.8 us -> 27.8 us
  between operations: 15.6 us -> 1.11 us
    psum x1 -> x0, waiting for transfers between devices: 95 us -> none  [from_root(): return lax.psum(kept, axis)]
    all_gather x1 -> x0, waiting for transfers between devices: 42.2 us -> none  [shards(): whole = lax.all_gather(own, 'dev', axis=0, tiled=True)]
    pallas_call x0 -> x3, Pallas kernels: none -> 36.8 us  [the longest x2 30.8 us: block(): pl.pallas_call(functools.partial(block_kernel, unit, len(sources)), out_s...]
    another operation x23 -> x5, other arithmetic: 35.9 us -> 5.26 us  [the longest x2 5.01 us: mixing_weights(): return jnp.stack(columns, axis=0)]
    dot_general x16 -> x0, matrix products: 20 us -> none  [cross_block(): result = jnp.dot(flat, table, preferred_element_type=jnp.float32)]
    ppermute x4 -> x9, starting transfers between devices: 11.7 us -> 27.8 us  [the longest x7 21.3 us: send(): return lax.ppermute(value, AXES, pairs(groups, devs, move))]
    squeeze x16 -> x0, local copies, waits for them, and re-layouts: 15.5 us -> none  [shards(): corr = lax.map(lambda block: cross_block(block, own, table), grouped)]
    unnamed x12 -> x19, local copies, waits for them, and re-layouts: 1.95 us -> 16.5 us
  transfers between devices with their start and end apart: 6 -> 9, of which waited for: 5 -> 3; matrix products, arithmetic and copies ran while one was open for 7% -> 15% of each run, Pallas kernels for 0% -> 22%
where the time goes in v1:
time: 113 us; the launch traced here: 112 us
  Pallas kernels  36.8 us (33%)
  starting transfers between devices  27.8 us (25%)
  local copies, waits for them, and re-layouts  25.5 us (23%)
  waiting for transfers between devices  11.8 us (10%)
  other arithmetic  9.27 us (8%)
    pallas_call x2, Pallas kernels, block(): pl.pallas_call(functools.partial(block_kernel, unit, len(sources)), out_s...  30.8 us
    ppermute x7, starting transfers between devices, send(): return lax.ppermute(value, AXES, pairs(groups, devs, move))  21.3 us
    unnamed x19, local copies, waits for them, and re-layouts  16.5 us
    ppermute x7, waiting for transfers between devices, send(): return lax.ppermute(value, AXES, pairs(groups, devs, move))  11.4 us
    pallas_call x1, Pallas kernels, make_weights(): pl.pallas_call(weights_kernel, out_shape=pltpu.VMEM((count * lags, bins),...  6 us
    another operation x2, other arithmetic, mixing_weights(): return jnp.stack(columns, axis=0)  5.01 us
    ppermute x1, starting transfers between devices, shards(): lax.ppermute(packed(shard - width), AXES, [(i, i + 1) for i in range(tota...  4.51 us
  transfers between devices with their start and end apart: 9, of which 3 were waited for; matrix products, arithmetic and copies ran while one was open for 15% of the time, Pallas kernels for 22%

profile of v1, /device:TPU:1, one launch (start us, length us, event | category | flops | bytes accessed | tf_op | source)
XLA Modules:
  0.0 112.2 jit_solution(17682193082984595993)
XLA Ops:
  0.6 1.2 %fusion.28 = (bf16[16,1,2048]{2,1,0:T(2,128)(2,1)S(1)}, bf16[16,1,2048]{2,1,0:T(2,128)(2,1)S(1)}) fusion(bf16[16,2,2048]{2,1,0:T(2,128)(2,1)} %param.6), kind=kLoop, calls=%fused_computation.80 | loop fusion | bytes 262144 | tf_op jit(solution)/shard_map/slice | solution.py:19
  1.9 0.1 fusion.4
  2.0 3.2 %collective-permute-start.1 = (bf16[16,4096]{1,0:T(8,128)(2,1)S(1)}, bf16[16,4096]{1,0:T(8,128)(2,1)S(1)}, u32[]{:S(2)}, u32[]{:S(2)}) collective-permute-start(bf16[16,4096]{1,0:T(8,128)(2,1)S(1)} %get-tuple-element.16), channel_id=1, source_target_pairs={{0,8},{1,9},{2,10},{3,11},{4,12},{5,13},{6,14},{7,15},{8,0},{9,1},... | collective-permute-start | bytes 393224 | tf_op jit(solution)/shard_map/ppermute | solution.py:227
  5.2 1.3 %collective-permute-start = (bf16[16,4096]{1,0:T(8,128)(2,1)S(1)}, bf16[16,4096]{1,0:T(8,128)(2,1)S(1)}, u32[]{:S(2)}, u32[]{:S(2)}) collective-permute-start(bf16[16,4096]{1,0:T(8,128)(2,1)S(1)} %get-tuple-element.16), channel_id=1, source_target_pairs={{0,4},{1,5},{2,6},{3,7},{4,8},{5,9},{6,10},{7,11},{8,12},{9,13},{1... | collective-permute-start | bytes 393224 | tf_op jit(solution)/shard_map/ppermute | solution.py:227
  6.5 2.0 %collective-permute-start.2 = (bf16[16,4096]{1,0:T(8,128)(2,1)S(1)}, bf16[16,4096]{1,0:T(8,128)(2,1)S(1)}, u32[]{:S(2)}, u32[]{:S(2)}) collective-permute-start(bf16[16,4096]{1,0:T(8,128)(2,1)S(1)} %get-tuple-element.16), channel_id=1, source_target_pairs={{0,12},{1,13},{2,14},{3,15},{4,0},{5,1},{6,2},{7,3},{8,4},{9,5},{1... | collective-permute-start | bytes 393224 | tf_op jit(solution)/shard_map/ppermute | solution.py:227
  8.5 0.8 fusion.27
  9.3 2.0 %fusion.26 = (bf16[2,256,4,128]{3,2,1,0:T(4,128)(2,1)S(1)}, bf16[2,256,4,128]{3,2,1,0:T(4,128)(2,1)S(1)}) fusion(bf16[2,256,16,128]{3,2,1,0:T(8,128)(2,1)} %param.7), kind=kLoop, calls=%fused_computation.78 | loop fusion | bytes 2097152 | tf_op jit(solution)/shard_map/slice | solution.py:275
  11.3 0.8 pad_maximum_fusion.2
  12.1 4.5 %collective-permute-start.7 = (bf16[2176,128]{1,0:T(8,128)(2,1)}, bf16[2176,128]{1,0:T(8,128)(2,1)S(1)}, u32[]{:S(2)}, u32[]{:S(2)}) collective-permute-start(bf16[2176,128]{1,0:T(8,128)(2,1)} %pad_maximum_fusion.2), channel_id=1, source_target_pairs={{0,1},{1,2},{2,3},{3,4},{4,5},{5,6},{6,7},{7,8},{8,9},{9,10},{10,1... | collective-permute-start | bytes 1671176 | tf_op jit(solution)/shard_map/ppermute | solution.py:279
  16.7 0.8 pad_maximum_fusion.1
  17.5 1.9 %collective-permute-start.6 = (bf16[2176,128]{1,0:T(8,128)(2,1)}, bf16[2176,128]{1,0:T(8,128)(2,1)}, u32[]{:S(2)}, u32[]{:S(2)}) collective-permute-start(bf16[2176,128]{1,0:T(8,128)(2,1)} %pad_maximum_fusion.1), channel_id=1, source_target_pairs={{1,0},{2,1},{3,2},{4,3},{5,4},{6,5},{7,6},{8,7},{9,8},{10,9},{11,1... | collective-permute-start | bytes 1671176 | tf_op jit(solution)/shard_map/ppermute | solution.py:280
  19.9 0.7 fusion.31
  20.9 3.7 %fusion.25 = (f32[1,16]{1,0:T(1,128)S(1)}, f32[1,16]{1,0:T(1,128)S(1)}, f32[1,16]{1,0:T(1,128)S(1)}, f32[1,16]{1,0:T(1,128)S(1)}, f32[1,16]{1,0:T(1,128)S(1)}, /*index=5*/f32[1,16]{1,0:T(1,128)S(1)}) fusion(s32[24]{0:T(128)S(1)} %convert_reduce_fusion, f32[]{:T(128)} %bitcast.32, f32[]{:T(128)} %bitcast.30, f32[]{:T(128)} %bitcast.28, f32[]{:T(128)} %bitcast.26, ...), kind=kLoop, calls=%fused_computation.74 | loop fusion | flops 192 | bytes 856 | tf_op jit(solution)/shard_map/stack | solution.py:47
  24.7 1.3 %fusion.19 = (f32[1,16]{1,0:T(1,128)S(1)}, f32[1,16]{1,0:T(1,128)S(1)}) fusion(s32[24]{0:T(128)S(1)} %convert_reduce_fusion, f32[]{:T(128)} %bitcast.19, f32[]{:T(128)} %bitcast.17), kind=kLoop, calls=%fused_computation.68 | loop fusion | flops 64 | bytes 328 | tf_op jit(solution)/shard_map/stack | solution.py:47
  25.9 0.7 eq.91
  26.8 0.9 pad_maximum_fusion.3
  27.6 1.2 %collective-permute-start.3 = (bf16[64,4096]{1,0:T(8,128)(2,1)}, bf16[64,4096]{1,0:T(8,128)(2,1)}, u32[]{:S(2)}, u32[]{:S(2)}) collective-permute-start(bf16[64,4096]{1,0:T(8,128)(2,1)} %pad_maximum_fusion.3), channel_id=1, source_target_pairs={{0,2},{1,17},{2,0},{3,19},{4,6},{5,21},{6,4},{7,23},{8,10},{9,25},... | collective-permute-start | bytes 1572872 | tf_op jit(solution)/shard_map/ppermute | solution.py:227
  28.9 0.4 collective-permute-done.7
  29.4 6.9 %collective-permute-done.3 = bf16[64,4096]{1,0:T(8,128)(2,1)} collective-permute-done((bf16[64,4096]{1,0:T(8,128)(2,1)}, bf16[64,4096]{1,0:T(8,128)(2,1)}, u32[]{:S(2)}, u32[]{:S(2)}) %collective-permute-start.3) | collective-permute-done | bytes 524320 | tf_op jit(solution)/shard_map/ppermute | solution.py:227
  36.3 1.1 constant_dynamic-update-slice_fusion.refs_0_
  37.4 0.2 collective-permute-start.4
  37.6 0.8 slice.135
  38.4 1.1 slice.141
  39.5 7.3 %collective-permute-start.8 = (bf16[128,4096]{1,0:T(8,128)(2,1)S(1)}, bf16[128,4096]{1,0:T(8,128)(2,1)S(1)}, u32[]{:S(2)}, u32[]{:S(2)}) collective-permute-start(bf16[128,4096]{1,0:T(8,128)(2,1)S(1)} %constant_dynamic-update-slice_fusion.refs_0_), channel_id=1, source_target_pairs={{0,1},{1,0},{2,3},{3,2},{4,5},{5,4},{6,7},{7,6},{8,9},{9,8},{10,11... | collective-permute-start | bytes 3145736 | tf_op jit(solution)/shard_map/ppermute | solution.py:227
  46.9 4.5 %collective-permute-done.4.refs_0_ = bf16[128,4096]{1,0:T(8,128)(2,1)S(1)} collective-permute-done((bf16[128,4096]{1,0:T(8,128)(2,1)S(1)}, bf16[128,4096]{1,0:T(8,128)(2,1)S(1)}, u32[]{:S(2)}, u32[]{:S(2)}) %collective-permute-start.4) | collective-permute-done | bytes 1048608 | tf_op jit(solution)/shard_map/ppermute | solution.py:227
  51.4 6.2 %collective-permute-start.5 = (bf16[128,4096]{1,0:T(8,128)(2,1)S(1)}, bf16[128,4096]{1,0:T(8,128)(2,1)S(1)}, u32[]{:S(2)}, u32[]{:S(2)}) collective-permute-start(bf16[128,4096]{1,0:T(8,128)(2,1)S(1)} %collective-permute-done.4.refs_0_), channel_id=1, source_target_pairs={{0,1},{1,0},{2,3},{3,2},{4,5},{5,4},{6,7},{7,6},{8,9},{9,8},{10,11... | collective-permute-start | bytes 3145736 | tf_op jit(solution)/shard_map/ppermute | solution.py:227
  57.6 6.0 %make_weights.1.refs_2_ = bf16[3072,4096]{1,0:T(8,128)(2,1)S(1)} custom-call(bf16[24,4096]{1,0:T(8,128)(2,1)S(1)} %maximum_maximum_fusion.receivers, bf16[128,4096]{1,0:T(8,128)(2,1)S(1)} %copy-done.2), custom_call_target="tpu_custom_call" | custom-call | flops 37748736 | bytes 25165824 | tf_op jit(solution)/shard_map/make_weights/pallas_call | solution.py:73
  63.6 8.3 %copy-done = bf16[3072,4096]{1,0:T(8,128)(2,1)} copy-done((bf16[3072,4096]{1,0:T(8,128)(2,1)}, bf16[3072,4096]{1,0:T(8,128)(2,1)S(1)}, u32[]{:S(2)}) %copy-start) | copy-done | bytes 25165848
  71.9 1.2 %pad_maximum_fusion.refs_3_ = bf16[2,256,24,128]{3,2,1,0:T(8,128)(2,1)S(1)} fusion(bf16[2,256,4,128]{3,2,1,0:T(4,128)(2,1)S(1)} %bitcast.120, bf16[2,256,4,128]{3,2,1,0:T(4,128)(2,1)S(1)} %bitcast.121, bf16[2,256,16,128]{3,2,1,0:T(8,128)(2,1)S(1)} %copy-done.3), kind=kLoop, calls=%fused_computation | loop fusion | flops 9437184 | bytes 6291456 | tf_op jit(solution)/shard_map/concatenate | solution.py:288
  73.3 8.2 %copy-done.1 = bf16[3072,4096]{1,0:T(8,128)(2,1)S(1)} copy-done((bf16[3072,4096]{1,0:T(8,128)(2,1)S(1)}, bf16[3072,4096]{1,0:T(8,128)(2,1)}, u32[]{:S(2)}) %copy-start.1) | copy-done | bytes 25165848
  81.4 18.7 %block.2 = (f32[2,256,16,128]{3,2,1,0:T(8,128)}, f32[2,256,16,128]{3,2,1,0:T(8,128)}) custom-call(s32[34]{0:T(128)S(1)} %get-tuple-element.28.info, f32[9,16,128]{2,1,0:T(8,128)S(1)} %broadcast_in_dim.2.mix, bf16[128,4096]{1,0:T(8,128)(2,1)S(1)} %constant_dynamic-update-slice_fusion.refs_0_, bf16[128,4096]{1,0:T(8,128)(2,1)S(1)} %collective-permute-done.8.refs_1_, ...), custom_call_target="tpu_custom_call" | custom-call | flops 6442450944 | bytes 4194304 | tf_op jit(solution)/shard_map/block/pallas_call | solution.py:178
  100.1 12.1 %block.3 = (f32[2,256,16,128]{3,2,1,0:T(8,128)}, f32[2,256,16,128]{3,2,1,0:T(8,128)}) custom-call(s32[34]{0:T(128)S(1)} %get-tuple-element.29.info, f32[9,16,128]{2,1,0:T(8,128)S(1)} %broadcast_in_dim.2.mix, bf16[128,4096]{1,0:T(8,128)(2,1)S(1)} %collective-permute-done.4.refs_0_, ...), custom_call_target="tpu_custom_call", output_to_operand_aliasing={{0}: (6, {}), {1}: (7, {})} | custom-call | flops 6442450944 | bytes 4194304 | tf_op jit(solution)/shard_map/block/pallas_call | solution.py:178
  (48 shorter events, 1.2 us)
Async XLA Ops:
  0.6 19.3 %copy-start.5 = (f32[9]{0:T(128)S(1)}, f32[9]{0:T(128)}, u32[]{:S(2)}) copy-start(f32[9]{0:T(128)} %param.10) | copy-start | bytes 112
  0.6 20.0 %copy-start.6 = (s32[16]{0:T(128)S(1)}, s32[16]{0:T(128)}, u32[]{:S(2)}) copy-start(s32[16]{0:T(128)} %param.9) | copy-start | bytes 196
  1.9 24.8 %copy-start.7 = (s32[2]{0:T(128)S(1)}, s32[2]{0:T(128)}, u32[]{:S(2)}) copy-start(s32[2]{0:T(128)} %param.8) | copy-start | bytes 28
  2.0 24.8 %collective-permute-start.1 = (bf16[16,4096]{1,0:T(8,128)(2,1)S(1)}, bf16[16,4096]{1,0:T(8,128)(2,1)S(1)}, u32[]{:S(2)}, u32[]{:S(2)}) collective-permute-start(bf16[16,4096]{1,0:T(8,128)(2,1)S(1)} %get-tuple-element.16), channel_id=1, source_target_pairs={{0,8},{1,9},{2,10},{3,11},{4,12},{5,13},{6,14},{7,15},{8,0},{9,1},... | collective-permute-start | bytes 393224 | tf_op jit(solution)/shard_map/ppermute | solution.py:227
  5.2 21.6 %collective-permute-start = (bf16[16,4096]{1,0:T(8,128)(2,1)S(1)}, bf16[16,4096]{1,0:T(8,128)(2,1)S(1)}, u32[]{:S(2)}, u32[]{:S(2)}) collective-permute-start(bf16[16,4096]{1,0:T(8,128)(2,1)S(1)} %get-tuple-element.16), channel_id=1, source_target_pairs={{0,4},{1,5},{2,6},{3,7},{4,8},{5,9},{6,10},{7,11},{8,12},{9,13},{1... | collective-permute-start | bytes 393224 | tf_op jit(solution)/shard_map/ppermute | solution.py:227
  6.5 20.3 %collective-permute-start.2 = (bf16[16,4096]{1,0:T(8,128)(2,1)S(1)}, bf16[16,4096]{1,0:T(8,128)(2,1)S(1)}, u32[]{:S(2)}, u32[]{:S(2)}) collective-permute-start(bf16[16,4096]{1,0:T(8,128)(2,1)S(1)} %get-tuple-element.16), channel_id=1, source_target_pairs={{0,12},{1,13},{2,14},{3,15},{4,0},{5,1},{6,2},{7,3},{8,4},{9,5},{1... | collective-permute-start | bytes 393224 | tf_op jit(solution)/shard_map/ppermute | solution.py:227
  12.1 17.3 %collective-permute-start.7 = (bf16[2176,128]{1,0:T(8,128)(2,1)}, bf16[2176,128]{1,0:T(8,128)(2,1)S(1)}, u32[]{:S(2)}, u32[]{:S(2)}) collective-permute-start(bf16[2176,128]{1,0:T(8,128)(2,1)} %pad_maximum_fusion.2), channel_id=1, source_target_pairs={{0,1},{1,2},{2,3},{3,4},{4,5},{5,6},{6,7},{7,8},{8,9},{9,10},{10,1... | collective-permute-start | bytes 1671176 | tf_op jit(solution)/shard_map/ppermute | solution.py:279
  17.5 20.1 %collective-permute-start.6 = (bf16[2176,128]{1,0:T(8,128)(2,1)}, bf16[2176,128]{1,0:T(8,128)(2,1)}, u32[]{:S(2)}, u32[]{:S(2)}) collective-permute-start(bf16[2176,128]{1,0:T(8,128)(2,1)} %pad_maximum_fusion.1), channel_id=1, source_target_pairs={{1,0},{2,1},{3,2},{4,3},{5,4},{6,5},{7,6},{8,7},{9,8},{10,9},{11,1... | collective-permute-start | bytes 1671176 | tf_op jit(solution)/shard_map/ppermute | solution.py:280
  19.8 37.8 %copy-start.2 = (bf16[128,4096]{1,0:T(8,128)(2,1)S(1)}, bf16[128,4096]{1,0:T(8,128)(2,1)}, u32[]{:S(2)}) copy-start(bf16[128,4096]{1,0:T(8,128)(2,1)} %constant.197.clone.table) | copy-start | bytes 3145732
  27.6 8.6 %collective-permute-start.3 = (bf16[64,4096]{1,0:T(8,128)(2,1)}, bf16[64,4096]{1,0:T(8,128)(2,1)}, u32[]{:S(2)}, u32[]{:S(2)}) collective-permute-start(bf16[64,4096]{1,0:T(8,128)(2,1)} %pad_maximum_fusion.3), channel_id=1, source_target_pairs={{0,2},{1,17},{2,0},{3,19},{4,6},{5,21},{6,4},{7,23},{8,10},{9,25},... | collective-permute-start | bytes 1572872 | tf_op jit(solution)/shard_map/ppermute | solution.py:227
  29.4 6.9 %copy-start.4 = (bf16[2176,128]{1,0:T(8,128)(2,1)}, bf16[2176,128]{1,0:T(8,128)(2,1)S(1)}, u32[]{:S(2)}) copy-start(bf16[2176,128]{1,0:T(8,128)(2,1)S(1)} %collective-permute-done.7) | copy-start | bytes 1671172
  37.4 14.0 %collective-permute-start.4 = (bf16[128,4096]{1,0:T(8,128)(2,1)S(1)}, bf16[128,4096]{1,0:T(8,128)(2,1)S(1)}, u32[]{:S(2)}, u32[]{:S(2)}) collective-permute-start(bf16[128,4096]{1,0:T(8,128)(2,1)S(1)} %constant_dynamic-update-slice_fusion.refs_0_), channel_id=1, source_target_pairs={{0,16},{1,3},{2,18},{3,1},{4,20},{5,7},{6,22},{7,5},{8,24},{9,11},... | collective-permute-start | bytes 3145736 | tf_op jit(solution)/shard_map/ppermute | solution.py:227
  39.5 33.6 %collective-permute-start.8 = (bf16[128,4096]{1,0:T(8,128)(2,1)S(1)}, bf16[128,4096]{1,0:T(8,128)(2,1)S(1)}, u32[]{:S(2)}, u32[]{:S(2)}) collective-permute-start(bf16[128,4096]{1,0:T(8,128)(2,1)S(1)} %constant_dynamic-update-slice_fusion.refs_0_), channel_id=1, source_target_pairs={{0,1},{1,0},{2,3},{3,2},{4,5},{5,4},{6,7},{7,6},{8,9},{9,8},{10,11... | collective-permute-start | bytes 3145736 | tf_op jit(solution)/shard_map/ppermute | solution.py:227
  51.4 48.7 %collective-permute-start.5 = (bf16[128,4096]{1,0:T(8,128)(2,1)S(1)}, bf16[128,4096]{1,0:T(8,128)(2,1)S(1)}, u32[]{:S(2)}, u32[]{:S(2)}) collective-permute-start(bf16[128,4096]{1,0:T(8,128)(2,1)S(1)} %collective-permute-done.4.refs_0_), channel_id=1, source_target_pairs={{0,1},{1,0},{2,3},{3,2},{4,5},{5,4},{6,7},{7,6},{8,9},{9,8},{10,11... | collective-permute-start | bytes 3145736 | tf_op jit(solution)/shard_map/ppermute | solution.py:227
  57.6 14.3 %copy-start.3 = (bf16[2,256,16,128]{3,2,1,0:T(8,128)(2,1)S(1)}, bf16[2,256,16,128]{3,2,1,0:T(8,128)(2,1)}, u32[]{:S(2)}) copy-start(bf16[2,256,16,128]{3,2,1,0:T(8,128)(2,1)} %param.7) | copy-start | bytes 6291460
  57.6 14.3 %slice-start = ((bf16[2176,128]{1,0:T(8,128)(2,1)}), bf16[2048,128]{1,0:T(8,128)(2,1)S(1)}, s32[]{:S(2)}) async-start(bf16[2176,128]{1,0:T(8,128)(2,1)} %copy-done.4), calls=%async_computation | async-start | bytes 1048576 | tf_op jit(solution)/shard_map/slice | solution.py:283
  63.6 8.3 %copy-start = (bf16[3072,4096]{1,0:T(8,128)(2,1)}, bf16[3072,4096]{1,0:T(8,128)(2,1)S(1)}, u32[]{:S(2)}) copy-start(bf16[3072,4096]{1,0:T(8,128)(2,1)S(1)} %make_weights.1.refs_2_) | copy-start | bytes 75497472
  73.3 8.2 %copy-start.1 = (bf16[3072,4096]{1,0:T(8,128)(2,1)S(1)}, bf16[3072,4096]{1,0:T(8,128)(2,1)}, u32[]{:S(2)}) copy-start(bf16[3072,4096]{1,0:T(8,128)(2,1)} %copy-done) | copy-start | bytes 75497472

commit v2 on v1

v2 whole, which is shorter than its diff:
```python
import functools
import math

import jax
import jax.numpy as jnp
import ml_dtypes
import numpy as np
from jax import lax
from jax.experimental import pallas as pl
from jax.experimental.pallas import tpu as pltpu
from jax.sharding import PartitionSpec as P

AXES = ("grp", "dev")
FILL = 512
SLOTS = 8


def whiten(spectra):
    real_part = spectra[:, 0, :].astype(jnp.float32)
    imag_part = spectra[:, 1, :].astype(jnp.float32)
    magnitude = jnp.sqrt(real_part * real_part + imag_part * imag_part)
    factor = 1.0 / jnp.maximum(magnitude, 0.25)
    pair = jnp.concatenate([real_part * factor, imag_part * factor], axis=1)
    return pair.astype(jnp.bfloat16)


def make_table(freqs, lags):
    bins = np.arange(freqs, dtype=np.int64)[None, :]
    shifts = np.arange(lags, dtype=np.int64)[:, None] - lags // 2
    modulus = (bins * shifts) % (2 * freqs)
    angle = modulus.astype(np.float64) * (math.pi / freqs)
    table = np.concatenate([np.cos(angle), -np.sin(angle)], axis=1) / math.sqrt(freqs)
    return jnp.asarray(table.astype(np.float32).astype(ml_dtypes.bfloat16))


def segment_of(channel_ids, seg_lengths):
    bounds = jnp.cumsum(seg_lengths)[:-1]
    return jnp.sum((channel_ids[:, None] >= bounds[None, :]).astype(jnp.int32), axis=1)


def mixing_weights(seg_ids, taps, count):
    width = (taps.shape[0] - 1) // 2
    centre = seg_ids[width : width + count]
    columns = []
    for offset in range(taps.shape[0]):
        same = (seg_ids[offset : offset + count] == centre).astype(jnp.float32)
        columns.append(taps[offset] * same)
    return jnp.stack(columns, axis=0)


def weights_kernel(receivers, table, weights):
    count, lags, freqs = receivers.shape[0], table.shape[0], table.shape[1] // 2
    fill = min(FILL, freqs)

    def body(step, _):
        first = pl.multiple_of(step * fill, fill)
        low, high = pl.ds(first, fill), pl.ds(freqs + first, fill)
        cosine = table[:, low].astype(jnp.float32)
        sine = table[:, high].astype(jnp.float32)
        for c in range(count):
            real_part = receivers[pl.ds(c, 1), low].astype(jnp.float32)
            imag_part = receivers[pl.ds(c, 1), high].astype(jnp.float32)
            rows = pl.ds(c * lags, lags)
            weights[rows, low] = (real_part * cosine - imag_part * sine).astype(jnp.bfloat16)
            weights[rows, high] = (imag_part * cosine + real_part * sine).astype(jnp.bfloat16)
        return 0

    lax.fori_loop(0, freqs // fill, body, 0)


def make_weights(receivers, table):
    count, bins = receivers.shape
    lags = table.shape[0]
    return pl.pallas_call(
        weights_kernel,
        out_shape=pltpu.VMEM((count * lags, bins), jnp.bfloat16),
        in_specs=[pl.BlockSpec(memory_space=pltpu.VMEM)] * 2,
        out_specs=pl.BlockSpec(memory_space=pltpu.VMEM),
        compiler_params=pltpu.CompilerParams(vmem_limit_bytes=8 << 20),
        cost_estimate=pl.CostEstimate(
            flops=3 * count * lags * bins, bytes_accessed=2 * count * lags * bins, transcendentals=0
        ),
        name="make_weights",
    )(receivers, table)


def edge_weights_kernel(first, high, low, table, weights, white):
    lags, freqs = table.shape[0], table.shape[1] // 2
    lanes = high.shape[1]
    half = freqs // lanes
    count = (high.shape[0] - first) // (2 * half)
    for side, edges in enumerate((high, low)):
        for c in range(count):
            at = first + c * 2 * half
            real_part = edges[pl.ds(at, half), :].astype(jnp.float32)
            imag_part = edges[pl.ds(at + half, half), :].astype(jnp.float32)
            magnitude = jnp.sqrt(real_part * real_part + imag_part * imag_part)
            factor = 1.0 / jnp.maximum(magnitude, 0.25)
            to = (side * count + c) * 2 * half
            for part, row in ((real_part, to), (imag_part, to + half)):
                rounded = (part * factor).astype(jnp.bfloat16)
                white[pl.ds(row, half), :] = rounded.astype(jnp.float32)

    def body(step, _):
        at = pl.multiple_of(step * lanes, lanes)
        low_bins, high_bins = pl.ds(at, lanes), pl.ds(freqs + at, lanes)
        cosine = table[:, low_bins].astype(jnp.float32)
        sine = table[:, high_bins].astype(jnp.float32)
        for c in range(2 * count):
            real_part = white[pl.ds(c * 2 * half + step, 1), :]
            imag_part = white[pl.ds(c * 2 * half + half + step, 1), :]
            rows = pl.ds(c * lags, lags)
            weights[rows, low_bins] = (real_part * cosine - imag_part * sine).astype(jnp.bfloat16)
            weights[rows, high_bins] = (imag_part * cosine + real_part * sine).astype(jnp.bfloat16)
        return 0

    lax.fori_loop(0, half, body, 0)


def make_edge_weights(high, low, first, count, table):
    lags, bins = table.shape
    return pl.pallas_call(
        functools.partial(edge_weights_kernel, first),
        out_shape=pltpu.VMEM((2 * count * lags, bins), jnp.bfloat16),
        in_specs=[pl.BlockSpec(memory_space=pltpu.VMEM)] * 3,
        out_specs=pl.BlockSpec(memory_space=pltpu.VMEM),
        scratch_shapes=[pltpu.VMEM((2 * (high.shape[0] - first), high.shape[1]), jnp.float32)],
        compiler_params=pltpu.CompilerParams(vmem_limit_bytes=8 << 20),
        cost_estimate=pl.CostEstimate(
            flops=6 * count * lags * bins, bytes_accessed=4 * count * lags * bins, transcendentals=0
        ),
        name="make_edge_weights",
    )(high, low, table)


def block_kernel(unit, parts, info, mix, *refs):
    sources = refs[:parts]
    weights_own, weights_edge, kept_own, kept_edge = refs[parts : parts + 4]
    stack_out, filtered_out = refs[-7], refs[-6]
    lhs, corr, stack_buf, filtered_buf, sems = refs[-5:]
    rows = lhs.shape[0]
    units = rows // unit
    steps, _, edges, lags = kept_edge.shape
    taps, shard, _ = mix.shape
    reach = shard + edges
    slots = stack_buf.shape[0]
    width = (taps - 1) // 2
    first = 0
    for part in sources:
        lhs[pl.ds(first, part.shape[0]), :] = part[...]
        first += part.shape[0]
    group = 4
    columns = group * lags

    def product(weights, base):
        def body(step, _):
            at = pl.multiple_of(step * columns, columns)
            out = lax.dot_general(
                lhs[...],
                weights[pl.ds(at, columns), :],
                (((1,), (1,)), ((), ())),
                preferred_element_type=jnp.float32,
            )
            for j in range(group):
                channel = base + step * group + j
                corr[pl.ds(channel, rows, stride=reach), :] = out[:, j * lags : (j + 1) * lags]
            return 0

        lax.fori_loop(0, weights.shape[0] // columns, body, 0)

    product(weights_own, 0)
    product(weights_edge, shard)

    def copies(slot, step, row):
        return (
            pltpu.make_async_copy(
                stack_buf.at[slot], stack_out.at[step, pl.ds(row, unit)], sems.at[0, slot]
            ),
            pltpu.make_async_copy(
                filtered_buf.at[slot], filtered_out.at[step, pl.ds(row, unit)], sems.at[1, slot]
            ),
        )

    def finish(slot):
        for copy in copies(slot, 0, 0):
            copy.wait()

    def visit(number, used):
        u, step = number // steps, number % steps
        row = info[steps + units + u]

        def work(used):
            slot = used % slots

            @pl.when(used >= slots)
            def _():
                finish(slot)

            for i in range(unit):
                at = pl.multiple_of((u * unit + i) * reach, 8)
                near = corr[pl.ds(at, shard), :] + kept_own[step, row + i].astype(jnp.float32)
                edge = corr[pl.ds(at + shard, edges), :] + kept_edge[step, row + i].astype(jnp.float32)
                whole = jnp.concatenate([near, edge], axis=0)
                stack_buf[slot, i] = near
                total = mix[width] * near
                for offset in range(-width, width + 1):
                    if offset:
                        moved = pltpu.roll(whole, (-offset) % reach, 0)[:shard]
                        total = total + mix[width + offset] * moved
                filtered_buf[slot, i] = total
            for copy in copies(slot, step, row):
                copy.start()
            return used + 1

        return lax.cond(info[step] == info[steps + u], work, lambda used: used, used)

    used = lax.fori_loop(0, units * steps, visit, 0)

    def drain(slot, _):
        @pl.when(slot < used)
        def _():
            finish(slot)

        return 0

    lax.fori_loop(0, slots, drain, 0)


def block(sources, weights, kept, mix, info, unit, outs, out_shape):
    rows = sum(part.shape[0] for part in sources)
    steps, count, edges, lags = kept[1].shape
    taps, shard, _ = mix.shape
    reach = shard + edges
    bins = weights[0].shape[1]
    vmem, anywhere = pl.BlockSpec(memory_space=pltpu.VMEM), pl.BlockSpec(memory_space=pl.ANY)
    carried = list(outs)
    before = 2 + len(sources) + 4
    return pl.pallas_call(
        functools.partial(block_kernel, unit, len(sources)),
        out_shape=(out_shape, out_shape),
        in_specs=[pl.BlockSpec(memory_space=pltpu.SMEM)]
        + [vmem] * (1 + len(sources) + 4)
        + [anywhere] * len(carried),
        out_specs=(anywhere, anywhere),
        scratch_shapes=[
            pltpu.VMEM((rows, bins), jnp.bfloat16),
            pltpu.VMEM((rows * reach, lags), jnp.float32),
            pltpu.VMEM((SLOTS, unit, shard, lags), jnp.float32),
            pltpu.VMEM((SLOTS, unit, shard, lags), jnp.float32),
            pltpu.SemaphoreType.DMA((2, SLOTS)),
        ],
        input_output_aliases={before: 0, before + 1: 1} if carried else {},
        compiler_params=pltpu.CompilerParams(vmem_limit_bytes=12 << 20),
        cost_estimate=pl.CostEstimate(
            flops=2 * rows * bins * reach * lags,
            bytes_accessed=8 * rows * shard * lags,
            transcendentals=0,
        ),
        name="block",
    )(info, mix, *sources, *weights, *kept, *carried)


def pairs(groups, devs, move):
    lines = devs // 4
    listed = []
    for g in range(groups):
        for line in range(lines):
            for side in range(2):
                for core in range(2):
                    h, other, flank, die = move(g, line, side, core)
                    listed.append(
                        (
                            g * devs + (line * 2 + side) * 2 + core,
                            h * devs + (other * 2 + flank) * 2 + die,
                        )
                    )
    return listed


def routes():
    groups, devs = lax.axis_size("grp"), lax.axis_size("dev")
    lines = devs // 4

    def send(value, move):
        return lax.ppermute(value, AXES, pairs(groups, devs, move))

    def along(value):
        return [
            send(value, lambda h, n, s, c, k=k: (h, (n + k) % lines, s, c)) for k in range(1, lines)
        ]

    def second(value):
        return send(value, lambda h, n, s, c: (h, n, 1 - s, c) if c == 0 else (1 - h, n, s, c))

    def third(value):
        return send(value, lambda h, n, s, c: (h, n, 1 - s, c) if c == 1 else (1 - h, n, s, c))

    def across(value):
        return send(value, lambda h, n, s, c: (h, n, s, 1 - c))

    return along, second, third, across


def owners(core, far):
    devs = lax.axis_size("dev")
    lines = devs // 4
    g, d = lax.axis_index("grp"), lax.axis_index("dev")
    line, side = d // 4, (d // 2) % 2
    j = jnp.arange(2, dtype=jnp.int32)[:, None]
    k = jnp.arange(lines, dtype=jnp.int32)[None, :]
    flip_side = jnp.where(core == 0, j, far)
    flip_group = jnp.where(core == 0, far, j)
    at_group, at_side = jnp.bitwise_xor(g, flip_group), jnp.bitwise_xor(side, flip_side)
    at_line = (line - k + lines) % lines
    return (at_group * devs + (at_line * 2 + at_side) * 2 + core).reshape(-1)


def shards(spectra, stack_in, plan, seg_lengths, taps):
    shard, _, freqs = spectra.shape
    steps, source_count, _, lags = stack_in.shape
    width = (taps.shape[0] - 1) // 2
    groups, devs = lax.axis_size("grp"), lax.axis_size("dev")
    total = groups * devs
    group_channels = devs * shard
    reach = shard + 2 * width
    everything = groups == 2 and devs % 4 == 0 and total * shard == 2 * source_count
    table = make_table(freqs, lags)

    own = whiten(spectra)
    along, second, third, across = routes()
    if everything:
        held = along(own)

    edge = steps * source_count * width

    def packed(first):
        stacks = lax.slice_in_dim(stack_in, first, first + width, axis=2)
        raw = lax.slice_in_dim(spectra, first, first + width, axis=0)
        return jnp.concatenate([stacks.reshape(edge, lags), raw.reshape(-1, lags)], axis=0)

    low = lax.ppermute(packed(shard - width), AXES, [(i, i + 1) for i in range(total - 1)])
    high = lax.ppermute(packed(0), AXES, [(i + 1, i) for i in range(total - 1)])

    def stacks_of(edges):
        return edges[:edge].reshape(steps, source_count, width, lags)

    start_channel = lax.axis_index(AXES) * shard
    channel_ids = start_channel + jnp.arange(reach, dtype=jnp.int32) - width
    mixing = mixing_weights(segment_of(channel_ids, seg_lengths), taps, shard)
    mix = jnp.broadcast_to(mixing[:, :, None], mixing.shape + (lags,))

    weights_own = make_weights(own, table)
    if everything:
        held, weights_own, mix = lax.optimization_barrier((held, weights_own, mix))
        first = jnp.concatenate([own] + held, axis=0)
        passed = second(first)
    kept_edge = jnp.concatenate([stacks_of(high), stacks_of(low)], axis=2)
    weights_edge = make_edge_weights(high, low, edge, width, table)
    weights, kept = (weights_own, weights_edge), (stack_in, kept_edge)

    out_shape = jax.ShapeDtypeStruct((steps, source_count, shard, lags), jnp.float32)

    def info_of(plan, channels):
        info = jnp.concatenate([plan, channels // source_count, channels % source_count])
        return info.astype(jnp.int32)

    if everything:
        core = lax.axis_index("dev") % 2
        near_info = info_of(plan, jnp.concatenate([owners(core, 0), owners(1 - core, 0)]) * shard)
        far_info = info_of(plan, jnp.concatenate([owners(core, 1), owners(1 - core, 1)]) * shard)
        passed, weights_edge, kept_edge, near_info, far_info = lax.optimization_barrier(
            (passed, weights_edge, kept_edge, near_info, far_info)
        )
        weights, kept = (weights_own, weights_edge), (stack_in, kept_edge)
        near = jnp.concatenate([first, passed], axis=0)
        far = third(near)
        near_other = across(near)
        outs = block((near, near_other), weights, kept, mix, near_info, shard, (), out_shape)
        far, outs = lax.optimization_barrier((far, outs))
        far_other = across(far)
        return block((far, far_other), weights, kept, mix, far_info, shard, outs, out_shape)
    outs = ()
    for step in range(steps):
        first = plan[step] * source_count
        mine = jnp.where(lax.axis_index("grp") == first // group_channels, own, 0)
        piece = lax.psum(mine.astype(own.dtype), "grp")
        whole = lax.all_gather(piece, "dev", axis=0, tiled=True)
        sources = lax.dynamic_slice_in_dim(whole, first % group_channels, source_count, 0)
        rows = step * source_count + jnp.arange(0, source_count, shard, dtype=jnp.int32)
        info = info_of(jnp.arange(steps, dtype=jnp.int32), rows)
        outs = block((sources,), weights, kept, mix, info, shard, outs, out_shape)
    return outs


def solution(mesh):
    placed = (P(AXES, None, None), P(None, None, AXES, None), P(), P(), P())
    return jax.shard_map(
        shards,
        mesh=mesh,
        in_specs=placed,
        out_specs=(P(None, None, AXES, None), P(None, None, AXES, None)),
        check_vma=False,
    )
```

time: 113 us -> 73.7 us (0.65)
  local copies, waits for them, and re-layouts: 25.5 us -> 8.97 us
  starting transfers between devices: 27.8 us -> 15.9 us
  waiting for transfers between devices: 11.8 us -> 4.39 us
  Pallas kernels: 36.8 us -> 33.5 us
    unnamed x19 -> x13, local copies, waits for them, and re-layouts: 16.5 us -> 2.78 us
    ppermute x7, starting transfers between devices: 21.3 us -> 9.47 us  [send(): return lax.ppermute(value, AXES, pairs(groups, devs, move))]
    ppermute x7, waiting for transfers between devices: 11.4 us -> 4.38 us  [send(): return lax.ppermute(value, AXES, pairs(groups, devs, move))]
    pallas_call x2, Pallas kernels: 30.8 us -> 25.6 us  [block(): pl.pallas_call(functools.partial(block_kernel, unit, len(sources)), out_s...]
    pallas_call x0 -> x1, Pallas kernels: none -> 3.92 us  [make_edge_weights(): pl.pallas_call(functools.partial(edge_weights_kernel, first), out_shape=p...]
    pallas_call x1, Pallas kernels: 6 us -> 4.03 us  [make_weights(): pl.pallas_call(weights_kernel, out_shape=pltpu.VMEM((count * lags, bins),...]
    ppermute x1, starting transfers between devices: 4.51 us -> 3 us  [shards(): lax.ppermute(packed(shard - width), AXES, [(i, i + 1) for i in range(tota...]
    ppermute x1, starting transfers between devices: 1.91 us -> 3.41 us  [shards(): high = lax.ppermute(packed(0), AXES, [(i + 1, i) for i in range(total - 1)])]
  transfers between devices with their start and end apart: 9 -> 9, of which waited for: 3 -> 3; matrix products, arithmetic and copies ran while one was open for 15% -> 23% of each run, Pallas kernels for 22% -> 29%
where the time goes in v2:
time: 73.7 us; the launch traced here: 72.6 us
  Pallas kernels  33.5 us (45%)
  starting transfers between devices  15.9 us (22%)
  local copies, waits for them, and re-layouts  8.97 us (12%)
  other arithmetic  8.92 us (12%)
  waiting for transfers between devices  4.39 us (6%)
  between operations  0.96 us (1%)
    pallas_call x2, Pallas kernels, block(): pl.pallas_call(functools.partial(block_kernel, unit, len(sources)), out_s...  25.6 us
    ppermute x7, starting transfers between devices, send(): return lax.ppermute(value, AXES, pairs(groups, devs, move))  9.47 us
    another operation x2, other arithmetic, mixing_weights(): return jnp.stack(columns, axis=0)  4.97 us
    ppermute x7, waiting for transfers between devices, send(): return lax.ppermute(value, AXES, pairs(groups, devs, move))  4.38 us
    pallas_call x1, Pallas kernels, make_weights(): pl.pallas_call(weights_kernel, out_shape=pltpu.VMEM((count * lags, bins),...  4.03 us
    pallas_call x1, Pallas kernels, make_edge_weights(): pl.pallas_call(functools.partial(edge_weights_kernel, first), out_shape=p...  3.92 us
    ppermute x1, starting transfers between devices, shards(): high = lax.ppermute(packed(0), AXES, [(i + 1, i) for i in range(total - 1)])  3.41 us
    ppermute x1, starting transfers between devices, shards(): lax.ppermute(packed(shard - width), AXES, [(i, i + 1) for i in range(tota...  3 us
  transfers between devices with their start and end apart: 9, of which 3 were waited for; matrix products, arithmetic and copies ran while one was open for 23% of the time, Pallas kernels for 29%

profile of v2, /device:TPU:1, one launch (start us, length us, event | category | flops | bytes accessed | tf_op | source)
XLA Modules:
  0.0 72.6 jit_solution(12295621430391347317)
XLA Ops:
  0.6 1.2 %fusion.30 = (bf16[16,1,2048]{2,1,0:T(2,128)(2,1)S(1)}, bf16[16,1,2048]{2,1,0:T(2,128)(2,1)S(1)}) fusion(bf16[16,2,2048]{2,1,0:T(2,128)(2,1)} %param.6), kind=kLoop, calls=%fused_computation.86 | loop fusion | bytes 262144 | tf_op jit(solution)/shard_map/slice | solution.py:20
  1.8 0.1 fusion.4
  2.0 4.2 %collective-permute-start.2 = (bf16[16,4096]{1,0:T(8,128)(2,1)S(1)}, bf16[16,4096]{1,0:T(8,128)(2,1)}, u32[]{:S(2)}, u32[]{:S(2)}) collective-permute-start(bf16[16,4096]{1,0:T(8,128)(2,1)S(1)} %get-tuple-element.41.receivers), channel_id=1, source_target_pairs={{0,12},{1,13},{2,14},{3,15},{4,0},{5,1},{6,2},{7,3},{8,4},{9,5},{1... | collective-permute-start | bytes 393224 | tf_op jit(solution)/shard_map/ppermute | solution.py:285
  6.2 0.5 collective-permute-start
  6.6 0.8 %fusion.29 = (bf16[4,2,2048]{2,1,0:T(2,128)(2,1)S(1)}, bf16[4,2,2048]{2,1,0:T(2,128)(2,1)S(1)}) fusion(bf16[16,2,2048]{2,1,0:T(2,128)(2,1)} %param.6), kind=kLoop, calls=%fused_computation.85 | loop fusion | bytes 131072 | tf_op jit(solution)/shard_map/slice | solution.py:338
  7.5 2.0 %fusion.28 = (bf16[2,256,4,128]{3,2,1,0:T(4,128)(2,1)S(1)}, bf16[2,256,4,128]{3,2,1,0:T(4,128)(2,1)S(1)}) fusion(bf16[2,256,16,128]{3,2,1,0:T(8,128)(2,1)} %refs_4_.3), kind=kLoop, calls=%fused_computation.84 | loop fusion | bytes 2097152 | tf_op jit(solution)/shard_map/slice | solution.py:337
  9.6 0.8 %pad_maximum_fusion.1 = bf16[2176,128]{1,0:T(8,128)(2,1)} fusion(bf16[128,128]{1,0:T(8,128)(2,1)S(1)} %reshape.171, bf16[2048,128]{1,0:T(8,128)(2,1)S(1)} %bitcast.47), kind=kLoop, calls=%fused_computation.1 | loop fusion | flops 1114112 | bytes 1114112 | tf_op jit(solution)/shard_map/concatenate | solution.py:339
  10.4 3.4 %collective-permute-start.4 = (bf16[2176,128]{1,0:T(8,128)(2,1)}, bf16[2176,128]{1,0:T(8,128)(2,1)S(1)}, u32[]{:S(2)}, u32[]{:S(2)}) collective-permute-start(bf16[2176,128]{1,0:T(8,128)(2,1)} %pad_maximum_fusion.1), channel_id=1, source_target_pairs={{1,0},{2,1},{3,2},{4,3},{5,4},{6,5},{7,6},{8,7},{9,8},{10,9},{11,1... | collective-permute-start | bytes 1671176 | tf_op jit(solution)/shard_map/ppermute | solution.py:342
  13.9 0.8 %pad_maximum_fusion.2 = bf16[2176,128]{1,0:T(8,128)(2,1)} fusion(bf16[128,128]{1,0:T(8,128)(2,1)S(1)} %reshape.173, bf16[2048,128]{1,0:T(8,128)(2,1)S(1)} %bitcast.44), kind=kLoop, calls=%fused_computation.2 | loop fusion | flops 1114112 | bytes 1114112 | tf_op jit(solution)/shard_map/concatenate | solution.py:339
  14.7 3.0 %collective-permute-start.5 = (bf16[2176,128]{1,0:T(8,128)(2,1)}, bf16[2176,128]{1,0:T(8,128)(2,1)S(1)}, u32[]{:S(2)}, u32[]{:S(2)}) collective-permute-start(bf16[2176,128]{1,0:T(8,128)(2,1)} %pad_maximum_fusion.2), channel_id=1, source_target_pairs={{0,1},{1,2},{2,3},{3,4},{4,5},{5,6},{6,7},{7,8},{8,9},{9,10},{10,1... | collective-permute-start | bytes 1671176 | tf_op jit(solution)/shard_map/ppermute | solution.py:341
  18.4 0.7 fusion.31
  19.2 0.1 slice_reduce_fusion
  19.4 0.1 convert_reduce_fusion
  19.5 1.2 %fusion.19 = (f32[1,16]{1,0:T(1,128)S(1)}, f32[1,16]{1,0:T(1,128)S(1)}) fusion(s32[24]{0:T(128)S(1)} %convert_reduce_fusion, f32[]{:T(128)} %bitcast.7, f32[]{:T(128)} %bitcast.5), kind=kLoop, calls=%fused_computation.70 | loop fusion | flops 64 | bytes 328 | tf_op jit(solution)/shard_map/stack | solution.py:48
  20.7 3.7 %fusion.25 = (f32[1,16]{1,0:T(1,128)S(1)}, f32[1,16]{1,0:T(1,128)S(1)}, f32[1,16]{1,0:T(1,128)S(1)}, f32[1,16]{1,0:T(1,128)S(1)}, f32[1,16]{1,0:T(1,128)S(1)}, /*index=5*/f32[1,16]{1,0:T(1,128)S(1)}) fusion(s32[24]{0:T(128)S(1)} %convert_reduce_fusion, f32[]{:T(128)} %bitcast.20, f32[]{:T(128)} %bitcast.18, f32[]{:T(128)} %bitcast.16, f32[]{:T(128)} %bitcast.14, ...), kind=kLoop, calls=%fused_computation.76 | loop fusion | flops 192 | bytes 856 | tf_op jit(solution)/shard_map/stack | solution.py:48
  24.5 0.6 eq.57
  25.2 4.0 %make_weights.1.refs_2_ = bf16[2048,4096]{1,0:T(8,128)(2,1)S(1)} custom-call(bf16[16,4096]{1,0:T(8,128)(2,1)S(1)} %get-tuple-element.41.receivers, bf16[128,4096]{1,0:T(8,128)(2,1)S(1)} %copy-done.1), custom_call_target="tpu_custom_call" | custom-call | flops 25165824 | bytes 16777216 | tf_op jit(solution)/shard_map/make_weights/pallas_call | solution.py:74
  29.4 0.9 %constant_dynamic-update-slice_fusion.3 = bf16[128,4096]{1,0:T(8,128)(2,1)S(1)} fusion(bf16[128,4096]{1,0:T(8,128)(2,1)S(1)} %get-tuple-element.40, bf16[16,4096]{1,0:T(8,128)(2,1)} %collective-permute-done), kind=kLoop, calls=%fused_computation.20 | loop fusion | bytes 262144
  30.3 1.1 %pad_maximum_fusion.3 = bf16[64,4096]{1,0:T(8,128)(2,1)S(1)} fusion(bf16[16,4096]{1,0:T(8,128)(2,1)} %collective-permute-done.2, bf16[16,4096]{1,0:T(8,128)(2,1)} %collective-permute-done.1, bf16[16,4096]{1,0:T(8,128)(2,1)} %collective-permute-done, bf16[16,2048]{1,0:T(8,128)(2,1)S(1)} %get-tuple-element.39, bf16[16,2048]{1,0:T(8,128)(2,1)S(1)} %get-tuple-element.38), kind=kLoop, calls=%fused_computation.3 | loop fusion | flops 2621440 | bytes 1048576 | tf_op jit(solution)/shard_map/concatenate | solution.py:355
  31.4 0.9 %constant_dynamic-update-slice_fusion.2 = bf16[128,4096]{1,0:T(8,128)(2,1)S(1)} fusion(bf16[128,4096]{1,0:T(8,128)(2,1)S(1)} %constant_dynamic-update-slice_fusion.3, bf16[16,4096]{1,0:T(8,128)(2,1)} %collective-permute-done.1), kind=kLoop, calls=%fused_computation.19 | loop fusion | bytes 262144
  32.3 1.3 %collective-permute-start.3 = (bf16[64,4096]{1,0:T(8,128)(2,1)S(1)}, bf16[64,4096]{1,0:T(8,128)(2,1)S(1)}, u32[]{:S(2)}, u32[]{:S(2)}) collective-permute-start(bf16[64,4096]{1,0:T(8,128)(2,1)S(1)} %pad_maximum_fusion.3), channel_id=1, source_target_pairs={{0,2},{1,17},{2,0},{3,19},{4,6},{5,21},{6,4},{7,23},{8,10},{9,25},... | collective-permute-start | bytes 1572872 | tf_op jit(solution)/shard_map/ppermute | solution.py:285
  33.6 0.9 %constant_dynamic-update-slice_fusion.1 = bf16[128,4096]{1,0:T(8,128)(2,1)S(1)} fusion(bf16[128,4096]{1,0:T(8,128)(2,1)S(1)} %constant_dynamic-update-slice_fusion.2, bf16[16,4096]{1,0:T(8,128)(2,1)} %collective-permute-done.2), kind=kLoop, calls=%fused_computation.18 | loop fusion | bytes 262144
  34.6 3.9 %make_edge_weights.1.refs_3_ = bf16[1024,4096]{1,0:T(8,128)(2,1)S(1)} custom-call(bf16[2176,128]{1,0:T(8,128)(2,1)S(1)} %collective-permute-done.4.high, bf16[2176,128]{1,0:T(8,128)(2,1)S(1)} %collective-permute-done.5.low, bf16[128,4096]{1,0:T(8,128)(2,1)S(1)} %copy-done.1), custom_call_target="tpu_custom_call" | custom-call | flops 12582912 | bytes 8388608 | tf_op jit(solution)/shard_map/make_edge_weights/pallas_call | solution.py:122
  38.6 0.5 pad_maximum_fusion.refs_5_
  39.1 1.5 %collective-permute-done.3 = bf16[64,4096]{1,0:T(8,128)(2,1)S(1)} collective-permute-done((bf16[64,4096]{1,0:T(8,128)(2,1)S(1)}, bf16[64,4096]{1,0:T(8,128)(2,1)S(1)}, u32[]{:S(2)}, u32[]{:S(2)}) %collective-permute-start.3) | collective-permute-done | bytes 524320 | tf_op jit(solution)/shard_map/ppermute | solution.py:285
  40.6 0.5 collective-permute-start.7
  41.1 1.7 %collective-permute-start.6 = (bf16[128,4096]{1,0:T(8,128)(2,1)S(1)}, bf16[128,4096]{1,0:T(8,128)(2,1)S(1)}, u32[]{:S(2)}, u32[]{:S(2)}) collective-permute-start(bf16[128,4096]{1,0:T(8,128)(2,1)S(1)} %constant_dynamic-update-slice_fusion.refs_0_), channel_id=1, source_target_pairs={{0,16},{1,3},{2,18},{3,1},{4,20},{5,7},{6,22},{7,5},{8,24},{9,11},... | collective-permute-start | bytes 3145736 | tf_op jit(solution)/shard_map/ppermute | solution.py:285
  42.7 0.6 collective-permute-done.7.refs_1_
  43.4 12.8 %block.2 = (f32[2,256,16,128]{3,2,1,0:T(8,128)}, f32[2,256,16,128]{3,2,1,0:T(8,128)}) custom-call(s32[34]{0:T(128)S(1)} %get-tuple-element.23.info, f32[9,16,128]{2,1,0:T(8,128)S(1)} %broadcast_in_dim.16.mix, bf16[128,4096]{1,0:T(8,128)(2,1)S(1)} %constant_dynamic-update-slice_fusion.refs_0_, bf16[128,4096]{1,0:T(8,128)(2,1)S(1)} %collective-permute-done.7.refs_1_, ...), custom_call_target="tpu_custom_call" | custom-call | flops 6442450944 | bytes 4194304 | tf_op jit(solution)/shard_map/block/pallas_call | solution.py:238
  56.2 1.4 %collective-permute-start.8 = (bf16[128,4096]{1,0:T(8,128)(2,1)S(1)}, bf16[128,4096]{1,0:T(8,128)(2,1)S(1)}, u32[]{:S(2)}, u32[]{:S(2)}) collective-permute-start(bf16[128,4096]{1,0:T(8,128)(2,1)S(1)} %collective-permute-done.6.refs_0_), channel_id=1, source_target_pairs={{0,1},{1,0},{2,3},{3,2},{4,5},{5,4},{6,7},{7,6},{8,9},{9,8},{10,11... | collective-permute-start | bytes 3145736 | tf_op jit(solution)/shard_map/ppermute | solution.py:285
  57.6 2.3 %collective-permute-done.8.refs_1_ = bf16[128,4096]{1,0:T(8,128)(2,1)S(1)} collective-permute-done((bf16[128,4096]{1,0:T(8,128)(2,1)S(1)}, bf16[128,4096]{1,0:T(8,128)(2,1)S(1)}, u32[]{:S(2)}, u32[]{:S(2)}) %collective-permute-start.8) | collective-permute-done | bytes 1048608 | tf_op jit(solution)/shard_map/ppermute | solution.py:285
  59.9 12.8 %block.3 = (f32[2,256,16,128]{3,2,1,0:T(8,128)}, f32[2,256,16,128]{3,2,1,0:T(8,128)}) custom-call(s32[34]{0:T(128)S(1)} %get-tuple-element.20.info, f32[9,16,128]{2,1,0:T(8,128)S(1)} %broadcast_in_dim.16.mix, bf16[128,4096]{1,0:T(8,128)(2,1)S(1)} %collective-permute-done.6.refs_0_, ...), custom_call_target="tpu_custom_call", output_to_operand_aliasing={{0}: (8, {}), {1}: (9, {})} | custom-call | flops 6442450944 | bytes 4194304 | tf_op jit(solution)/shard_map/block/pallas_call | solution.py:238
  (43 shorter events, 1.2 us)
Async XLA Ops:
  2.0 27.3 %collective-permute-start.2 = (bf16[16,4096]{1,0:T(8,128)(2,1)S(1)}, bf16[16,4096]{1,0:T(8,128)(2,1)}, u32[]{:S(2)}, u32[]{:S(2)}) collective-permute-start(bf16[16,4096]{1,0:T(8,128)(2,1)S(1)} %get-tuple-element.41.receivers), channel_id=1, source_target_pairs={{0,12},{1,13},{2,14},{3,15},{4,0},{5,1},{6,2},{7,3},{8,4},{9,5},{1... | collective-permute-start | bytes 393224 | tf_op jit(solution)/shard_map/ppermute | solution.py:285
  6.2 23.1 %collective-permute-start.1 = (bf16[16,4096]{1,0:T(8,128)(2,1)S(1)}, bf16[16,4096]{1,0:T(8,128)(2,1)}, u32[]{:S(2)}, u32[]{:S(2)}) collective-permute-start(bf16[16,4096]{1,0:T(8,128)(2,1)S(1)} %get-tuple-element.41.receivers), channel_id=1, source_target_pairs={{0,8},{1,9},{2,10},{3,11},{4,12},{5,13},{6,14},{7,15},{8,0},{9,1},... | collective-permute-start | bytes 393224 | tf_op jit(solution)/shard_map/ppermute | solution.py:285
  6.2 23.1 %collective-permute-start = (bf16[16,4096]{1,0:T(8,128)(2,1)S(1)}, bf16[16,4096]{1,0:T(8,128)(2,1)}, u32[]{:S(2)}, u32[]{:S(2)}) collective-permute-start(bf16[16,4096]{1,0:T(8,128)(2,1)S(1)} %get-tuple-element.41.receivers), channel_id=1, source_target_pairs={{0,4},{1,5},{2,6},{3,7},{4,8},{5,9},{6,10},{7,11},{8,12},{9,13},{1... | collective-permute-start | bytes 393224 | tf_op jit(solution)/shard_map/ppermute | solution.py:285
  7.5 10.9 %copy-start.2 = (f32[9]{0:T(128)S(1)}, f32[9]{0:T(128)}, u32[]{:S(2)}) copy-start(f32[9]{0:T(128)} %param.10) | copy-start | bytes 112
  7.5 11.6 %copy-start.3 = (s32[16]{0:T(128)S(1)}, s32[16]{0:T(128)}, u32[]{:S(2)}) copy-start(s32[16]{0:T(128)} %param.9) | copy-start | bytes 196
  7.5 17.6 %copy-start.1 = (bf16[128,4096]{1,0:T(8,128)(2,1)S(1)}, bf16[128,4096]{1,0:T(8,128)(2,1)}, u32[]{:S(2)}) copy-start(bf16[128,4096]{1,0:T(8,128)(2,1)} %constant.155.clone.table) | copy-start | bytes 3145732
  10.4 24.1 %collective-permute-start.4 = (bf16[2176,128]{1,0:T(8,128)(2,1)}, bf16[2176,128]{1,0:T(8,128)(2,1)S(1)}, u32[]{:S(2)}, u32[]{:S(2)}) collective-permute-start(bf16[2176,128]{1,0:T(8,128)(2,1)} %pad_maximum_fusion.1), channel_id=1, source_target_pairs={{1,0},{2,1},{3,2},{4,3},{5,4},{6,5},{7,6},{8,7},{9,8},{10,9},{11,1... | collective-permute-start | bytes 1671176 | tf_op jit(solution)/shard_map/ppermute | solution.py:342
  14.7 19.9 %collective-permute-start.5 = (bf16[2176,128]{1,0:T(8,128)(2,1)}, bf16[2176,128]{1,0:T(8,128)(2,1)S(1)}, u32[]{:S(2)}, u32[]{:S(2)}) collective-permute-start(bf16[2176,128]{1,0:T(8,128)(2,1)} %pad_maximum_fusion.2), channel_id=1, source_target_pairs={{0,1},{1,2},{2,3},{3,4},{4,5},{5,6},{6,7},{7,8},{8,9},{9,10},{10,1... | collective-permute-start | bytes 1671176 | tf_op jit(solution)/shard_map/ppermute | solution.py:341
  25.1 4.0 %copy-start.4 = (s32[2]{0:T(128)S(1)}, s32[2]{0:T(128)}, u32[]{:S(2)}) copy-start(s32[2]{0:T(128)} %param.8) | copy-start | bytes 28
  32.3 8.3 %collective-permute-start.3 = (bf16[64,4096]{1,0:T(8,128)(2,1)S(1)}, bf16[64,4096]{1,0:T(8,128)(2,1)S(1)}, u32[]{:S(2)}, u32[]{:S(2)}) collective-permute-start(bf16[64,4096]{1,0:T(8,128)(2,1)S(1)} %pad_maximum_fusion.3), channel_id=1, source_target_pairs={{0,2},{1,17},{2,0},{3,19},{4,6},{5,21},{6,4},{7,23},{8,10},{9,25},... | collective-permute-start | bytes 1572872 | tf_op jit(solution)/shard_map/ppermute | solution.py:285
  38.5 4.8 %copy-start = (bf16[2,256,16,128]{3,2,1,0:T(8,128)(2,1)S(1)}, bf16[2,256,16,128]{3,2,1,0:T(8,128)(2,1)}, u32[]{:S(2)}) copy-start(bf16[2,256,16,128]{3,2,1,0:T(8,128)(2,1)} %refs_4_.3) | copy-start | bytes 6291460
  40.6 2.7 %collective-permute-start.7 = (bf16[128,4096]{1,0:T(8,128)(2,1)S(1)}, bf16[128,4096]{1,0:T(8,128)(2,1)S(1)}, u32[]{:S(2)}, u32[]{:S(2)}) collective-permute-start(bf16[128,4096]{1,0:T(8,128)(2,1)S(1)} %constant_dynamic-update-slice_fusion.refs_0_), channel_id=1, source_target_pairs={{0,1},{1,0},{2,3},{3,2},{4,5},{5,4},{6,7},{7,6},{8,9},{9,8},{10,11... | collective-permute-start | bytes 3145736 | tf_op jit(solution)/shard_map/ppermute | solution.py:285
  41.1 15.1 %collective-permute-start.6 = (bf16[128,4096]{1,0:T(8,128)(2,1)S(1)}, bf16[128,4096]{1,0:T(8,128)(2,1)S(1)}, u32[]{:S(2)}, u32[]{:S(2)}) collective-permute-start(bf16[128,4096]{1,0:T(8,128)(2,1)S(1)} %constant_dynamic-update-slice_fusion.refs_0_), channel_id=1, source_target_pairs={{0,16},{1,3},{2,18},{3,1},{4,20},{5,7},{6,22},{7,5},{8,24},{9,11},... | collective-permute-start | bytes 3145736 | tf_op jit(solution)/shard_map/ppermute | solution.py:285
  56.2 3.7 %collective-permute-start.8 = (bf16[128,4096]{1,0:T(8,128)(2,1)S(1)}, bf16[128,4096]{1,0:T(8,128)(2,1)S(1)}, u32[]{:S(2)}, u32[]{:S(2)}) collective-permute-start(bf16[128,4096]{1,0:T(8,128)(2,1)S(1)} %collective-permute-done.6.refs_0_), channel_id=1, source_target_pairs={{0,1},{1,0},{2,3},{3,2},{4,5},{5,4},{6,7},{7,6},{8,9},{9,8},{10,11... | collective-permute-start | bytes 3145736 | tf_op jit(solution)/shard_map/ppermute | solution.py:285

commit v3 on v2

v3 whole, which is shorter than its diff:
```python
import functools
import math

import jax
import jax.numpy as jnp
import ml_dtypes
import numpy as np
from jax import lax
from jax.experimental import pallas as pl
from jax.experimental.pallas import tpu as pltpu
from jax.sharding import PartitionSpec as P

AXES = ("grp", "dev")
FILL = 512
SLOTS = 8


def whiten(spectra):
    real_part = spectra[:, 0, :].astype(jnp.float32)
    imag_part = spectra[:, 1, :].astype(jnp.float32)
    magnitude = jnp.sqrt(real_part * real_part + imag_part * imag_part)
    factor = 1.0 / jnp.maximum(magnitude, 0.25)
    pair = jnp.concatenate([real_part * factor, imag_part * factor], axis=1)
    return pair.astype(jnp.bfloat16)


def make_table(freqs, lags):
    bins = np.arange(freqs, dtype=np.int64)[None, :]
    shifts = np.arange(lags, dtype=np.int64)[:, None] - lags // 2
    modulus = (bins * shifts) % (2 * freqs)
    angle = modulus.astype(np.float64) * (math.pi / freqs)
    table = np.concatenate([np.cos(angle), -np.sin(angle)], axis=1) / math.sqrt(freqs)
    return jnp.asarray(table.astype(np.float32).astype(ml_dtypes.bfloat16))


VMEM = pl.BlockSpec(memory_space=pltpu.VMEM)
SMEM = pl.BlockSpec(memory_space=pltpu.SMEM)
ANY = pl.BlockSpec(memory_space=pl.ANY)


def mix_weights(seg_lengths, taps, mix):
    count, shard, lags = mix.shape
    width = (count - 1) // 2
    start = (lax.axis_index("grp") * lax.axis_size("dev") + lax.axis_index("dev")) * shard
    ids = start + lax.broadcasted_iota(jnp.int32, (shard, lags), 0)
    segs = [jnp.zeros((shard, lags), jnp.int32) for _ in range(count)]
    bound = 0
    for m in range(seg_lengths.shape[0] - 1):
        bound = bound + seg_lengths[m]
        for offset in range(count):
            segs[offset] += jnp.where(ids >= bound - (offset - width), 1, 0)
    for offset in range(count):
        mix[offset] = jnp.where(segs[offset] == segs[width], taps[offset], 0.0)


def weights_kernel(receivers, table, weights):
    count, lags, freqs = receivers.shape[0], table.shape[0], table.shape[1] // 2
    fill = min(FILL, freqs)

    def body(step, _):
        first = pl.multiple_of(step * fill, fill)
        low, high = pl.ds(first, fill), pl.ds(freqs + first, fill)
        cosine = table[:, low].astype(jnp.float32)
        sine = table[:, high].astype(jnp.float32)
        for c in range(count):
            real_part = receivers[pl.ds(c, 1), low].astype(jnp.float32)
            imag_part = receivers[pl.ds(c, 1), high].astype(jnp.float32)
            rows = pl.ds(c * lags, lags)
            weights[rows, low] = (real_part * cosine - imag_part * sine).astype(jnp.bfloat16)
            weights[rows, high] = (imag_part * cosine + real_part * sine).astype(jnp.bfloat16)
        return 0

    lax.fori_loop(0, freqs // fill, body, 0)


def make_weights(receivers, table):
    count, bins = receivers.shape
    lags = table.shape[0]
    return pl.pallas_call(
        weights_kernel,
        out_shape=pltpu.VMEM((count * lags, bins), jnp.bfloat16),
        in_specs=[VMEM, VMEM],
        out_specs=VMEM,
        compiler_params=pltpu.CompilerParams(vmem_limit_bytes=8 << 20),
        cost_estimate=pl.CostEstimate(
            flops=3 * count * lags * bins, bytes_accessed=2 * count * lags * bins, transcendentals=0
        ),
        name="make_weights",
    )(receivers, table)


def pack_kernel(width, own, stack_in, to_next, to_last, spread, rows):
    steps, sources, shard, lags = stack_in.shape
    unit = spread.shape[0] // shard
    groups = sources // unit
    sides = ((to_next, shard - width), (to_last, 0))

    def body(number, _):
        step, at = number // groups, pl.multiple_of(number % groups * unit, unit)
        spread[...] = stack_in[step, pl.ds(at, unit)].astype(jnp.float32).reshape(unit * shard, lags)
        for to, first in sides:
            for c in range(width):
                part = spread[pl.ds(first + c, unit, stride=shard), :]
                row = pl.multiple_of((step * width + c) * sources + at, unit)
                to[pl.ds(row, unit), :] = part.astype(jnp.bfloat16)
        return 0

    lax.fori_loop(0, steps * groups, body, 0)
    pieces = own.shape[1] // lags
    for to, first in sides:
        for j in range(pieces):
            part = own[:, j * lags : (j + 1) * lags].astype(jnp.float32)
            rows[pl.ds(j * width, width), :] = part[first : first + width]
        to[pl.ds(steps * width * sources, pieces * width), :] = rows[...].astype(jnp.bfloat16)


def pack(own, stack_in, width):
    steps, sources, shard, lags = stack_in.shape
    pieces = own.shape[1] // lags
    shape = jax.ShapeDtypeStruct((width * (steps * sources + pieces), lags), jnp.bfloat16)
    return pl.pallas_call(
        functools.partial(pack_kernel, width),
        out_shape=(shape, shape),
        in_specs=[VMEM, VMEM],
        out_specs=(VMEM, VMEM),
        scratch_shapes=[
            pltpu.VMEM((16 * shard, lags), jnp.float32),
            pltpu.VMEM((pieces * width, lags), jnp.float32),
        ],
        compiler_params=pltpu.CompilerParams(vmem_limit_bytes=8 << 20),
        cost_estimate=pl.CostEstimate(
            flops=0, bytes_accessed=2 * stack_in.size, transcendentals=0
        ),
        name="pack",
    )(own, stack_in)


def join_kernel(*refs):
    parts, out, sems = refs[:-2], refs[-2], refs[-1]
    copies, at = [], 0
    for number, part in enumerate(parts):
        to = out.at[pl.ds(at, part.shape[0])]
        copies.append(pltpu.make_async_copy(part, to, sems.at[number]))
        at += part.shape[0]
    for copy in copies:
        copy.start()
    for copy in copies:
        copy.wait()


def join(parts):
    rows = sum(part.shape[0] for part in parts)
    return pl.pallas_call(
        join_kernel,
        out_shape=pltpu.VMEM((rows, parts[0].shape[1]), parts[0].dtype),
        in_specs=[ANY] * len(parts),
        out_specs=VMEM,
        scratch_shapes=[pltpu.SemaphoreType.DMA((len(parts),))],
        compiler_params=pltpu.CompilerParams(vmem_limit_bytes=2 << 20),
        cost_estimate=pl.CostEstimate(
            flops=0, bytes_accessed=2 * rows * parts[0].shape[1], transcendentals=0
        ),
        name="join",
    )(*parts)


def edge_weights_kernel(first, high, low, table, weights, white):
    lags, freqs = table.shape[0], table.shape[1] // 2
    lanes = high.shape[1]
    pieces = 2 * freqs // lanes
    count = (high.shape[0] - first) // pieces
    size = pieces * count
    for side, edges in enumerate((high, low)):
        white[pl.ds(side * size, size), :] = edges[pl.ds(first, size), :].astype(jnp.float32)

    def body(step, _):
        at = pl.multiple_of(step * lanes, lanes)
        low_bins, high_bins = pl.ds(at, lanes), pl.ds(freqs + at, lanes)
        cosine = table[:, low_bins].astype(jnp.float32)
        sine = table[:, high_bins].astype(jnp.float32)
        for c in range(2 * count):
            row = c // count * size + step * count + c % count
            real_part = white[pl.ds(row, 1), :]
            imag_part = white[pl.ds(row + size // 2, 1), :]
            rows = pl.ds(c * lags, lags)
            weights[rows, low_bins] = (real_part * cosine - imag_part * sine).astype(jnp.bfloat16)
            weights[rows, high_bins] = (imag_part * cosine + real_part * sine).astype(jnp.bfloat16)
        return 0

    lax.fori_loop(0, pieces // 2, body, 0)


def make_edge_weights(high, low, first, count, table):
    lags, bins = table.shape
    return pl.pallas_call(
        functools.partial(edge_weights_kernel, first),
        out_shape=pltpu.VMEM((2 * count * lags, bins), jnp.bfloat16),
        in_specs=[VMEM] * 3,
        out_specs=VMEM,
        scratch_shapes=[pltpu.VMEM((2 * (high.shape[0] - first), high.shape[1]), jnp.float32)],
        compiler_params=pltpu.CompilerParams(vmem_limit_bytes=8 << 20),
        cost_estimate=pl.CostEstimate(
            flops=6 * count * lags * bins, bytes_accessed=4 * count * lags * bins, transcendentals=0
        ),
        name="make_edge_weights",
    )(high, low, table)


def block_kernel(unit, parts, locate, plan, seg_lengths, taps, *refs):
    sources = refs[:parts]
    weights_own, weights_edge, kept_own, high, low = refs[parts : parts + 5]
    stack_out, filtered_out = refs[-9], refs[-8]
    lhs, corr, mix, edge_buf, stack_buf, filtered_buf, sems = refs[-7:]
    rows = lhs.shape[0]
    units = rows // unit
    steps, count, shard, lags = kept_own.shape
    width = (taps.shape[0] - 1) // 2
    edges = 2 * width
    reach = shard + edges
    slots = stack_buf.shape[0]
    mix_weights(seg_lengths, taps, mix)
    first = 0
    for part in sources:
        lhs[pl.ds(first, part.shape[0]), :] = part[...]
        first += part.shape[0]
    group = 4
    columns = group * lags

    def product(weights, base):
        def body(step, _):
            at = pl.multiple_of(step * columns, columns)
            out = lax.dot_general(
                lhs[...],
                weights[pl.ds(at, columns), :],
                (((1,), (1,)), ((), ())),
                preferred_element_type=jnp.float32,
            )
            for j in range(group):
                channel = base + step * group + j
                corr[pl.ds(channel, rows, stride=reach), :] = out[:, j * lags : (j + 1) * lags]
            return 0

        lax.fori_loop(0, weights.shape[0] // columns, body, 0)

    product(weights_own, 0)
    product(weights_edge, shard)

    def copies(slot, step, row):
        return (
            pltpu.make_async_copy(
                stack_buf.at[slot], stack_out.at[step, pl.ds(row, unit)], sems.at[0, slot]
            ),
            pltpu.make_async_copy(
                filtered_buf.at[slot], filtered_out.at[step, pl.ds(row, unit)], sems.at[1, slot]
            ),
        )

    def finish(slot):
        for copy in copies(slot, 0, 0):
            copy.wait()

    def visit(number, used):
        u, step = number // steps, number % steps
        wanted, row = locate(u, step, plan)
        row = pl.multiple_of(row, unit)

        def work(used):
            slot = used % slots

            @pl.when(used >= slots)
            def _():
                finish(slot)

            for c in range(width):
                at = pl.multiple_of((step * width + c) * count + row, unit)
                edge_buf[pl.ds(c, unit, stride=edges), :] = high[pl.ds(at, unit), :].astype(jnp.float32)
                edge_buf[pl.ds(width + c, unit, stride=edges), :] = low[pl.ds(at, unit), :].astype(
                    jnp.float32
                )
            for i in range(unit):
                at = pl.multiple_of((u * unit + i) * reach, 8)
                near = corr[pl.ds(at, shard), :] + kept_own[step, row + i].astype(jnp.float32)
                edge = corr[pl.ds(at + shard, edges), :] + edge_buf[pl.ds(i * edges, edges), :]
                whole = jnp.concatenate([near, edge], axis=0)
                stack_buf[slot, i] = near
                total = mix[width] * near
                for offset in range(-width, width + 1):
                    if offset:
                        moved = pltpu.roll(whole, (-offset) % reach, 0)[:shard]
                        total = total + mix[width + offset] * moved
                filtered_buf[slot, i] = total
            for copy in copies(slot, step, row):
                copy.start()
            return used + 1

        return lax.cond(wanted, work, lambda used: used, used)

    used = lax.fori_loop(0, units * steps, visit, 0)

    def drain(slot, _):
        @pl.when(slot < used)
        def _():
            finish(slot)

        return 0

    lax.fori_loop(0, slots, drain, 0)


def block(sources, weights, kept, small, locate, outs, out_shape):
    rows = sum(part.shape[0] for part in sources)
    steps, count, shard, lags = kept[0].shape
    taps = small[2].shape[0]
    edges = taps - 1
    reach = shard + edges
    bins = weights[0].shape[1]
    carried = list(outs)
    before = 3 + len(sources) + 5
    return pl.pallas_call(
        functools.partial(block_kernel, shard, len(sources), locate),
        out_shape=(out_shape, out_shape),
        in_specs=[SMEM] * 3 + [VMEM] * (len(sources) + 5) + [ANY] * len(carried),
        out_specs=(ANY, ANY),
        scratch_shapes=[
            pltpu.VMEM((rows, bins), jnp.bfloat16),
            pltpu.VMEM((rows * reach, lags), jnp.float32),
            pltpu.VMEM((taps, shard, lags), jnp.float32),
            pltpu.VMEM((shard * edges, lags), jnp.float32),
            pltpu.VMEM((SLOTS, shard, shard, lags), jnp.float32),
            pltpu.VMEM((SLOTS, shard, shard, lags), jnp.float32),
            pltpu.SemaphoreType.DMA((2, SLOTS)),
        ],
        input_output_aliases={before: 0, before + 1: 1} if carried else {},
        compiler_params=pltpu.CompilerParams(vmem_limit_bytes=12 << 20),
        cost_estimate=pl.CostEstimate(
            flops=2 * rows * bins * reach * lags,
            bytes_accessed=8 * rows * shard * lags,
            transcendentals=0,
        ),
        name="block",
    )(*small, *sources, *weights, *kept, *carried)


def pairs(groups, devs, move):
    lines = devs // 4
    listed = []
    for g in range(groups):
        for line in range(lines):
            for side in range(2):
                for core in range(2):
                    h, other, flank, die = move(g, line, side, core)
                    listed.append(
                        (
                            g * devs + (line * 2 + side) * 2 + core,
                            h * devs + (other * 2 + flank) * 2 + die,
                        )
                    )
    return listed


def routes():
    groups, devs = lax.axis_size("grp"), lax.axis_size("dev")
    lines = devs // 4

    def send(value, move):
        return lax.ppermute(value, AXES, pairs(groups, devs, move))

    def along(value):
        return [
            send(value, lambda h, n, s, c, k=k: (h, (n + k) % lines, s, c)) for k in range(1, lines)
        ]

    def second(value):
        return send(value, lambda h, n, s, c: (h, n, 1 - s, c) if c == 0 else (1 - h, n, s, c))

    def third(value):
        return send(value, lambda h, n, s, c: (h, n, 1 - s, c) if c == 1 else (1 - h, n, s, c))

    def across(value):
        return send(value, lambda h, n, s, c: (h, n, s, 1 - c))

    return along, second, third, across


def locate_held(far, shard, source_count, u, step, plan):
    devs = lax.axis_size("dev")
    lines = devs // 4
    g, d = lax.axis_index("grp"), lax.axis_index("dev")
    line, side, core = d // 4, (d // 2) % 2, d % 2
    held, within = u // (2 * lines), u % (2 * lines)
    die = jnp.bitwise_xor(core, held)
    j, k = within // lines, within % lines
    at_side = jnp.bitwise_xor(side, jnp.where(die == 0, j, far))
    at_group = jnp.bitwise_xor(g, jnp.where(die == 0, far, j))
    at_line = (line - k + lines) % lines
    channel = (at_group * devs + (at_line * 2 + at_side) * 2 + die) * shard
    return channel // source_count == plan[step], channel % source_count


def locate_step(this, shard, u, step, plan):
    return step == this, u * shard


def shards(spectra, stack_in, plan, seg_lengths, taps):
    shard, _, freqs = spectra.shape
    steps, source_count, _, lags = stack_in.shape
    width = (taps.shape[0] - 1) // 2
    groups, devs = lax.axis_size("grp"), lax.axis_size("dev")
    total = groups * devs
    group_channels = devs * shard
    everything = groups == 2 and devs % 4 == 0 and total * shard == 2 * source_count
    table = make_table(freqs, lags)

    own = whiten(spectra)
    along, second, third, across = routes()
    if everything:
        held = along(own)

    to_next, to_last = pack(own, stack_in, width)
    low = lax.ppermute(to_next, AXES, [(i, i + 1) for i in range(total - 1)])
    high = lax.ppermute(to_last, AXES, [(i + 1, i) for i in range(total - 1)])
    weights_own = make_weights(own, table)
    small = (plan, seg_lengths, taps)
    if everything:
        held, weights_own = lax.optimization_barrier((held, weights_own))
        first = join([own] + held)
        passed = second(first)
    weights_edge = make_edge_weights(high, low, steps * width * source_count, width, table)
    out_shape = jax.ShapeDtypeStruct((steps, source_count, shard, lags), jnp.float32)
    if everything:
        passed, weights_edge = lax.optimization_barrier((passed, weights_edge))
        weights, kept = (weights_own, weights_edge), (stack_in, high, low)
        near = jnp.concatenate([first, passed], axis=0)
        far = third(near)
        near_other = across(near)
        outs = ()
        locate = functools.partial(locate_held, 0, shard, source_count)
        outs = block((near, near_other), weights, kept, small, locate, outs, out_shape)
        far, outs = lax.optimization_barrier((far, outs))
        far_other = across(far)
        locate = functools.partial(locate_held, 1, shard, source_count)
        return block((far, far_other), weights, kept, small, locate, outs, out_shape)
    weights, kept, outs = (weights_own, weights_edge), (stack_in, high, low), ()
    for step in range(steps):
        first = plan[step] * source_count
        mine = jnp.where(lax.axis_index("grp") == first // group_channels, own, 0)
        piece = lax.psum(mine.astype(own.dtype), "grp")
        whole = lax.all_gather(piece, "dev", axis=0, tiled=True)
        sources = lax.dynamic_slice_in_dim(whole, first % group_channels, source_count, 0)
        locate = functools.partial(locate_step, step, shard)
        outs = block((sources,), weights, kept, small, locate, outs, out_shape)
    return outs


def solution(mesh):
    placed = (P(AXES, None, None), P(None, None, AXES, None), P(), P(), P())
    return jax.shard_map(
        shards,
        mesh=mesh,
        in_specs=placed,
        out_specs=(P(None, None, AXES, None), P(None, None, AXES, None)),
        check_vma=False,
    )
```

time: 73.7 us -> 70.9 us (0.962)
  other arithmetic: 8.92 us -> 0.22 us
  waiting for transfers between devices: 4.39 us -> 12.1 us
  local copies, waits for them, and re-layouts: 8.97 us -> 4.04 us
  Pallas kernels: 33.5 us -> 37.4 us
    ppermute x2, waiting for transfers between devices: 0.01 us -> 9.57 us  [the longest x1 9.57 us: shards(): low = lax.ppermute(to_next, AXES, [(i, i + 1) for i in range(total - 1)])]
    another operation x4 -> x1, other arithmetic: 5.13 us -> 0.12 us  [the longest x2 4.97 us: mixing_weights(): return jnp.stack(columns, axis=0)]
    pallas_call x2 -> x4, Pallas kernels: 25.6 us -> 29.5 us  [the longest x2 27.5 us: block(): pl.pallas_call(functools.partial(block_kernel, shard, len(sources), locat...]
    slice x6 -> x0, local copies, waits for them, and re-layouts: 3.72 us -> none  [the longest x1 2.04 us: packed(): stacks = lax.slice_in_dim(stack_in, first, first + width, axis=2)]
    concatenate x5 -> x2, other arithmetic: 3.38 us -> 0.1 us  [the longest x1 0.09 us: shards(): near = jnp.concatenate([first, passed], axis=0)]
    ppermute x7, waiting for transfers between devices: 4.38 us -> 2.56 us  [send(): return lax.ppermute(value, AXES, pairs(groups, devs, move))]
    unnamed x13 -> x12, local copies, waits for them, and re-layouts: 2.78 us -> 2.84 us
  transfers between devices with their start and end apart: 9 -> 9, of which waited for: 3 -> 4; matrix products, arithmetic and copies ran while one was open for 23% -> 0% of each run, Pallas kernels for 29% -> 31%
where the time goes in v3:
time: 70.9 us; the launch traced here: 70.3 us
  Pallas kernels  37.4 us (53%)
  starting transfers between devices  15.7 us (22%)
  waiting for transfers between devices  12.1 us (17%)
  local copies, waits for them, and re-layouts  4.04 us (6%)
  between operations  0.8 us (1%)
    pallas_call x2, Pallas kernels, block(): pl.pallas_call(functools.partial(block_kernel, shard, len(sources), locat...  27.5 us
    ppermute x1, waiting for transfers between devices, shards(): low = lax.ppermute(to_next, AXES, [(i, i + 1) for i in range(total - 1)])  9.57 us
    ppermute x7, starting transfers between devices, send(): return lax.ppermute(value, AXES, pairs(groups, devs, move))  9.24 us
    pallas_call x1, Pallas kernels, make_weights(): pl.pallas_call(weights_kernel, out_shape=pltpu.VMEM((count * lags, bins),...  4.04 us
    pallas_call x1, Pallas kernels, make_edge_weights(): pl.pallas_call(functools.partial(edge_weights_kernel, first), out_shape=p...  3.89 us
    ppermute x1, starting transfers between devices, shards(): high = lax.ppermute(to_last, AXES, [(i + 1, i) for i in range(total - 1)])  3.42 us
    ppermute x1, starting transfers between devices, shards(): low = lax.ppermute(to_next, AXES, [(i, i + 1) for i in range(total - 1)])  3.02 us
    unnamed x12, local copies, waits for them, and re-layouts  2.84 us
  transfers between devices with their start and end apart: 9, of which 4 were waited for; matrix products, arithmetic and copies ran while one was open for 0% of the time, Pallas kernels for 31%

profile of v3, /device:TPU:1, one launch (start us, length us, event | category | flops | bytes accessed | tf_op | source)
XLA Modules:
  0.0 70.3 jit_solution(15747253962268741641)
XLA Ops:
  0.6 1.2 %fusion.6 = (bf16[16,1,2048]{2,1,0:T(2,128)(2,1)S(1)}, bf16[16,1,2048]{2,1,0:T(2,128)(2,1)S(1)}) fusion(bf16[16,2,2048]{2,1,0:T(2,128)(2,1)} %param.6), kind=kLoop, calls=%fused_computation.14 | loop fusion | bytes 262144 | tf_op jit(solution)/shard_map/slice | solution.py:20
  1.8 0.1 fusion.4
  2.0 4.2 %collective-permute-start.2 = (bf16[16,4096]{1,0:T(8,128)(2,1)S(1)}, bf16[16,4096]{1,0:T(8,128)(2,1)S(1)}, u32[]{:S(2)}, u32[]{:S(2)}) collective-permute-start(bf16[16,4096]{1,0:T(8,128)(2,1)S(1)} %pad_maximum_fusion.1.receivers.refs_0_.own), channel_id=1, source_target_pairs={{0,12},{1,13},{2,14},{3,15},{4,0},{5,1},{6,2},{7,3},{8,4},{9,5},{1... | collective-permute-start | bytes 393224 | tf_op jit(solution)/shard_map/ppermute | solution.py:366
  6.2 0.0 collective-permute-start.1
  6.2 0.5 collective-permute-start
  6.6 1.6 %copy-done = bf16[2,256,16,128]{3,2,1,0:T(8,128)(2,1)S(1)} copy-done((bf16[2,256,16,128]{3,2,1,0:T(8,128)(2,1)S(1)}, bf16[2,256,16,128]{3,2,1,0:T(8,128)(2,1)}, u32[]{:S(2)}) %copy-start) | copy-done | bytes 2097176
  8.2 1.2 %pack.1 = (bf16[2176,128]{1,0:T(8,128)(2,1)S(1)}, bf16[2176,128]{1,0:T(8,128)(2,1)S(1)}) custom-call(bf16[16,4096]{1,0:T(8,128)(2,1)S(1)} %pad_maximum_fusion.1.receivers.refs_0_.own, bf16[2,256,16,128]{3,2,1,0:T(8,128)(2,1)S(1)} %copy-done), custom_call_target="tpu_custom_call" | custom-call | bytes 2097152 | tf_op jit(solution)/shard_map/pack/pallas_call | solution.py:121
  9.4 3.4 %collective-permute-start.4 = (bf16[2176,128]{1,0:T(8,128)(2,1)S(1)}, bf16[2176,128]{1,0:T(8,128)(2,1)S(1)}, u32[]{:S(2)}, u32[]{:S(2)}) collective-permute-start(bf16[2176,128]{1,0:T(8,128)(2,1)S(1)} %get-tuple-element.18), channel_id=1, source_target_pairs={{1,0},{2,1},{3,2},{4,3},{5,4},{6,5},{7,6},{8,7},{9,8},{10,9},{11,1... | collective-permute-start | bytes 1671176 | tf_op jit(solution)/shard_map/ppermute | solution.py:421
  12.9 3.0 %collective-permute-start.5 = (bf16[2176,128]{1,0:T(8,128)(2,1)S(1)}, bf16[2176,128]{1,0:T(8,128)(2,1)S(1)}, u32[]{:S(2)}, u32[]{:S(2)}) collective-permute-start(bf16[2176,128]{1,0:T(8,128)(2,1)S(1)} %get-tuple-element.19), channel_id=1, source_target_pairs={{0,1},{1,2},{2,3},{3,4},{4,5},{5,6},{6,7},{7,8},{8,9},{9,10},{10,1... | collective-permute-start | bytes 1671176 | tf_op jit(solution)/shard_map/ppermute | solution.py:420
  15.9 0.0 copy-start.2
  15.9 1.2 %copy-done.2 = bf16[128,4096]{1,0:T(8,128)(2,1)S(1)} copy-done((bf16[128,4096]{1,0:T(8,128)(2,1)S(1)}, bf16[128,4096]{1,0:T(8,128)(2,1)}, u32[]{:S(2)}) %copy-start.2) | copy-done | bytes 1048600
  17.1 4.0 %make_weights.1.refs_2_ = bf16[2048,4096]{1,0:T(8,128)(2,1)S(1)} custom-call(bf16[16,4096]{1,0:T(8,128)(2,1)S(1)} %pad_maximum_fusion.1.receivers.refs_0_.own, bf16[128,4096]{1,0:T(8,128)(2,1)S(1)} %copy-done.2), custom_call_target="tpu_custom_call" | custom-call | flops 25165824 | bytes 16777216 | tf_op jit(solution)/shard_map/make_weights/pallas_call | solution.py:79
  21.2 0.0 collective-permute-done.2.refs_3_
  21.2 0.0 collective-permute-done.1.refs_2_
  21.2 0.0 collective-permute-done.refs_1_
  21.2 0.7 %join.1 = bf16[64,4096]{1,0:T(8,128)(2,1)S(1)} custom-call(bf16[16,4096]{1,0:T(8,128)(2,1)S(1)} %pad_maximum_fusion.1.receivers.refs_0_.own, bf16[16,4096]{1,0:T(8,128)(2,1)S(1)} %collective-permute-done.refs_1_, bf16[16,4096]{1,0:T(8,128)(2,1)S(1)} %collective-permute-done.1.refs_2_, bf16[16,4096]{1,0:T(8,128)(2,1)S(1)} %collective-permute-done.2.refs_3_), custom_call_target="tpu_custom_call" | custom-call | bytes 524288 | tf_op jit(solution)/shard_map/join/pallas_call | solution.py:153
  21.9 0.0 copy-start.1
  21.9 0.0 copy-start.3
  22.0 0.0 copy-start.4
  22.0 0.0 copy-start.5
  22.0 1.3 %collective-permute-start.3 = (bf16[64,4096]{1,0:T(8,128)(2,1)S(1)}, bf16[64,4096]{1,0:T(8,128)(2,1)S(1)}, u32[]{:S(2)}, u32[]{:S(2)}) collective-permute-start(bf16[64,4096]{1,0:T(8,128)(2,1)S(1)} %join.1), channel_id=1, source_target_pairs={{0,2},{1,17},{2,0},{3,19},{4,6},{5,21},{6,4},{7,23},{8,10},{9,25},... | collective-permute-start | bytes 1572872 | tf_op jit(solution)/shard_map/ppermute | solution.py:366
  23.3 9.6 %collective-permute-done.5.low.refs_6_ = bf16[2176,128]{1,0:T(8,128)(2,1)S(1)} collective-permute-done((bf16[2176,128]{1,0:T(8,128)(2,1)S(1)}, bf16[2176,128]{1,0:T(8,128)(2,1)S(1)}, u32[]{:S(2)}, u32[]{:S(2)}) %collective-permute-start.5) | collective-permute-done | bytes 557088 | tf_op jit(solution)/shard_map/ppermute | solution.py:420
  32.9 3.9 %make_edge_weights.1.refs_3_ = bf16[1024,4096]{1,0:T(8,128)(2,1)S(1)} custom-call(bf16[2176,128]{1,0:T(8,128)(2,1)S(1)} %collective-permute-done.4.high.refs_5_, bf16[2176,128]{1,0:T(8,128)(2,1)S(1)} %collective-permute-done.5.low.refs_6_, bf16[128,4096]{1,0:T(8,128)(2,1)S(1)} %copy-done.2), custom_call_target="tpu_custom_call" | custom-call | flops 12582912 | bytes 8388608 | tf_op jit(solution)/shard_map/make_edge_weights/pallas_call | solution.py:195
  36.8 0.1 pad_maximum_fusion.refs_0_
  36.9 0.1 collective-permute-start.7
  36.9 2.6 %collective-permute-start.6 = (bf16[128,4096]{1,0:T(8,128)(2,1)S(1)}, bf16[128,4096]{1,0:T(8,128)(2,1)S(1)}, u32[]{:S(2)}, u32[]{:S(2)}) collective-permute-start(bf16[128,4096]{1,0:T(8,128)(2,1)S(1)} %pad_maximum_fusion.refs_0_), channel_id=1, source_target_pairs={{0,16},{1,3},{2,18},{3,1},{4,20},{5,7},{6,22},{7,5},{8,24},{9,11},... | collective-permute-start | bytes 3145736 | tf_op jit(solution)/shard_map/ppermute | solution.py:366
  39.5 0.1 collective-permute-done.7.refs_1_
  39.6 12.0 %block.2 = (f32[2,256,16,128]{3,2,1,0:T(8,128)}, f32[2,256,16,128]{3,2,1,0:T(8,128)}) custom-call(s32[2]{0:T(128)S(1)} %copy-done.3, s32[16]{0:T(128)S(1)} %copy-done.4, f32[9]{0:T(128)S(1)} %copy-done.5, bf16[128,4096]{1,0:T(8,128)(2,1)S(1)} %pad_maximum_fusion.refs_0_, bf16[128,4096]{1,0:T(8,128)(2,1)S(1)} %collective-permute-done.7.refs_1_, ...), custom_call_target="tpu_custom_call" | custom-call | flops 6442450944 | bytes 4194304 | tf_op jit(solution)/shard_map/block/pallas_call | solution.py:319
  51.6 0.2 collective-permute-done.6.refs_0_
  51.8 0.6 collective-permute-start.8
  52.5 2.3 %collective-permute-done.8.refs_1_ = bf16[128,4096]{1,0:T(8,128)(2,1)S(1)} collective-permute-done((bf16[128,4096]{1,0:T(8,128)(2,1)S(1)}, bf16[128,4096]{1,0:T(8,128)(2,1)S(1)}, u32[]{:S(2)}, u32[]{:S(2)}) %collective-permute-start.8) | collective-permute-done | bytes 1048608 | tf_op jit(solution)/shard_map/ppermute | solution.py:366
  54.8 15.5 %block.3 = (f32[2,256,16,128]{3,2,1,0:T(8,128)}, f32[2,256,16,128]{3,2,1,0:T(8,128)}) custom-call(s32[2]{0:T(128)S(1)} %copy-done.3, s32[16]{0:T(128)S(1)} %copy-done.4, f32[9]{0:T(128)S(1)} %copy-done.5, bf16[128,4096]{1,0:T(8,128)(2,1)S(1)} %collective-permute-done.6.refs_0_, ...), custom_call_target="tpu_custom_call", output_to_operand_aliasing={{0}: (10, {}), {1}: (11, {})} | custom-call | flops 6442450944 | bytes 4194304 | tf_op jit(solution)/shard_map/block/pallas_call | solution.py:319
  (8 shorter events, 0.0 us)
Async XLA Ops:
  2.0 19.2 %collective-permute-start.2 = (bf16[16,4096]{1,0:T(8,128)(2,1)S(1)}, bf16[16,4096]{1,0:T(8,128)(2,1)S(1)}, u32[]{:S(2)}, u32[]{:S(2)}) collective-permute-start(bf16[16,4096]{1,0:T(8,128)(2,1)S(1)} %pad_maximum_fusion.1.receivers.refs_0_.own), channel_id=1, source_target_pairs={{0,12},{1,13},{2,14},{3,15},{4,0},{5,1},{6,2},{7,3},{8,4},{9,5},{1... | collective-permute-start | bytes 393224 | tf_op jit(solution)/shard_map/ppermute | solution.py:366
  6.2 15.0 %collective-permute-start.1 = (bf16[16,4096]{1,0:T(8,128)(2,1)S(1)}, bf16[16,4096]{1,0:T(8,128)(2,1)S(1)}, u32[]{:S(2)}, u32[]{:S(2)}) collective-permute-start(bf16[16,4096]{1,0:T(8,128)(2,1)S(1)} %pad_maximum_fusion.1.receivers.refs_0_.own), channel_id=1, source_target_pairs={{0,8},{1,9},{2,10},{3,11},{4,12},{5,13},{6,14},{7,15},{8,0},{9,1},... | collective-permute-start | bytes 393224 | tf_op jit(solution)/shard_map/ppermute | solution.py:366
  6.2 15.0 %collective-permute-start = (bf16[16,4096]{1,0:T(8,128)(2,1)S(1)}, bf16[16,4096]{1,0:T(8,128)(2,1)S(1)}, u32[]{:S(2)}, u32[]{:S(2)}) collective-permute-start(bf16[16,4096]{1,0:T(8,128)(2,1)S(1)} %pad_maximum_fusion.1.receivers.refs_0_.own), channel_id=1, source_target_pairs={{0,4},{1,5},{2,6},{3,7},{4,8},{5,9},{6,10},{7,11},{8,12},{9,13},{1... | collective-permute-start | bytes 393224 | tf_op jit(solution)/shard_map/ppermute | solution.py:366
  6.6 1.6 %copy-start = (bf16[2,256,16,128]{3,2,1,0:T(8,128)(2,1)S(1)}, bf16[2,256,16,128]{3,2,1,0:T(8,128)(2,1)}, u32[]{:S(2)}) copy-start(bf16[2,256,16,128]{3,2,1,0:T(8,128)(2,1)} %refs_4_.3) | copy-start | bytes 6291460
  9.4 13.8 %collective-permute-start.4 = (bf16[2176,128]{1,0:T(8,128)(2,1)S(1)}, bf16[2176,128]{1,0:T(8,128)(2,1)S(1)}, u32[]{:S(2)}, u32[]{:S(2)}) collective-permute-start(bf16[2176,128]{1,0:T(8,128)(2,1)S(1)} %get-tuple-element.18), channel_id=1, source_target_pairs={{1,0},{2,1},{3,2},{4,3},{5,4},{6,5},{7,6},{8,7},{9,8},{10,9},{11,1... | collective-permute-start | bytes 1671176 | tf_op jit(solution)/shard_map/ppermute | solution.py:421
  12.9 20.0 %collective-permute-start.5 = (bf16[2176,128]{1,0:T(8,128)(2,1)S(1)}, bf16[2176,128]{1,0:T(8,128)(2,1)S(1)}, u32[]{:S(2)}, u32[]{:S(2)}) collective-permute-start(bf16[2176,128]{1,0:T(8,128)(2,1)S(1)} %get-tuple-element.19), channel_id=1, source_target_pairs={{0,1},{1,2},{2,3},{3,4},{4,5},{5,6},{6,7},{7,8},{8,9},{9,10},{10,1... | collective-permute-start | bytes 1671176 | tf_op jit(solution)/shard_map/ppermute | solution.py:420
  15.9 1.2 %copy-start.2 = (bf16[128,4096]{1,0:T(8,128)(2,1)S(1)}, bf16[128,4096]{1,0:T(8,128)(2,1)}, u32[]{:S(2)}) copy-start(bf16[128,4096]{1,0:T(8,128)(2,1)} %constant.6.clone.table) | copy-start | bytes 3145732
  21.9 17.7 %copy-start.1 = (bf16[2,256,16,128]{3,2,1,0:T(8,128)(2,1)S(1)}, bf16[2,256,16,128]{3,2,1,0:T(8,128)(2,1)}, u32[]{:S(2)}) copy-start(bf16[2,256,16,128]{3,2,1,0:T(8,128)(2,1)} %refs_4_.3) | copy-start | bytes 6291460
  21.9 17.6 %copy-start.3 = (s32[2]{0:T(128)S(1)}, s32[2]{0:T(128)}, u32[]{:S(2)}) copy-start(s32[2]{0:T(128)} %plan.3) | copy-start | bytes 28
  22.0 17.6 %copy-start.4 = (s32[16]{0:T(128)S(1)}, s32[16]{0:T(128)}, u32[]{:S(2)}) copy-start(s32[16]{0:T(128)} %seg_lengths.3) | copy-start | bytes 196
  22.0 17.6 %copy-start.5 = (f32[9]{0:T(128)S(1)}, f32[9]{0:T(128)}, u32[]{:S(2)}) copy-start(f32[9]{0:T(128)} %taps.3) | copy-start | bytes 112
  22.0 14.8 %collective-permute-start.3 = (bf16[64,4096]{1,0:T(8,128)(2,1)S(1)}, bf16[64,4096]{1,0:T(8,128)(2,1)S(1)}, u32[]{:S(2)}, u32[]{:S(2)}) collective-permute-start(bf16[64,4096]{1,0:T(8,128)(2,1)S(1)} %join.1), channel_id=1, source_target_pairs={{0,2},{1,17},{2,0},{3,19},{4,6},{5,21},{6,4},{7,23},{8,10},{9,25},... | collective-permute-start | bytes 1572872 | tf_op jit(solution)/shard_map/ppermute | solution.py:366
  36.9 2.7 %collective-permute-start.7 = (bf16[128,4096]{1,0:T(8,128)(2,1)S(1)}, bf16[128,4096]{1,0:T(8,128)(2,1)S(1)}, u32[]{:S(2)}, u32[]{:S(2)}) collective-permute-start(bf16[128,4096]{1,0:T(8,128)(2,1)S(1)} %pad_maximum_fusion.refs_0_), channel_id=1, source_target_pairs={{0,1},{1,0},{2,3},{3,2},{4,5},{5,4},{6,7},{7,6},{8,9},{9,8},{10,11... | collective-permute-start | bytes 3145736 | tf_op jit(solution)/shard_map/ppermute | solution.py:366
  36.9 14.9 %collective-permute-start.6 = (bf16[128,4096]{1,0:T(8,128)(2,1)S(1)}, bf16[128,4096]{1,0:T(8,128)(2,1)S(1)}, u32[]{:S(2)}, u32[]{:S(2)}) collective-permute-start(bf16[128,4096]{1,0:T(8,128)(2,1)S(1)} %pad_maximum_fusion.refs_0_), channel_id=1, source_target_pairs={{0,16},{1,3},{2,18},{3,1},{4,20},{5,7},{6,22},{7,5},{8,24},{9,11},... | collective-permute-start | bytes 3145736 | tf_op jit(solution)/shard_map/ppermute | solution.py:366
  51.8 2.9 %collective-permute-start.8 = (bf16[128,4096]{1,0:T(8,128)(2,1)S(1)}, bf16[128,4096]{1,0:T(8,128)(2,1)S(1)}, u32[]{:S(2)}, u32[]{:S(2)}) collective-permute-start(bf16[128,4096]{1,0:T(8,128)(2,1)S(1)} %collective-permute-done.6.refs_0_), channel_id=1, source_target_pairs={{0,1},{1,0},{2,3},{3,2},{4,5},{5,4},{6,7},{7,6},{8,9},{9,8},{10,11... | collective-permute-start | bytes 3145736 | tf_op jit(solution)/shard_map/ppermute | solution.py:366
